TPU v7x, 32 devices: a whole 2x2x4 slice. The times are simulated.
32 devices in a mesh: dp: 4 (over x, core), gx: 2 (over y), gy: 4 (over z).
Axes of the slice: x: 2, y: 2, z: 4, core: 2. Of those that a mesh axis runs over, the one named last changes fastest.
Arguments:
- inputs: bfloat16 [4096, 960], P(('dp', 'gx', 'gy')), may hold values from -6 to 6
- segments: int32 [4096], P('dp'), may hold values from 0 to 15, never falling along the last dimension, each value on 1 to 512 neighbouring positions
- attn_gain: float32 [960], replicated, may hold values from 0.5 to 1.5
- query_weight: bfloat16 [960, 960], P('gx', 'gy'), may hold values from -1.6 to 1.6
- key_weight: bfloat16 [960, 320], P('gx', 'gy'), may hold values from -1.6 to 1.6
- value_weight: bfloat16 [960, 320], P('gx', 'gy'), may hold values from -0.1875 to 0.1875
- output_weight: bfloat16 [960, 960], P('gx', 'gy'), may hold values from -0.75 to 0.75
- mlp_gain: float32 [960], replicated, may hold values from 0.5 to 1.5
- gate_weight: bfloat16 [960, 2560], P('gx', 'gy'), may hold values from -0.1875 to 0.1875
- up_weight: bfloat16 [960, 2560], P('gx', 'gy'), may hold values from -0.1875 to 0.1875
- down_weight: bfloat16 [2560, 960], P('gx', 'gy'), may hold values from -0.125 to 0.125
- cotangent: bfloat16 [4096, 960], P(('dp', 'gx', 'gy')), may hold values from -6 to 6
Outputs:
- layer_out: bfloat16 [4096, 960], P(('dp', 'gx', 'gy'))
- input_grad: bfloat16 [4096, 960], P(('dp', 'gx', 'gy'))
- query_grad: float32 [960, 960], P('gx', 'gy')
- key_grad: float32 [960, 320], P('gx', 'gy')
- value_grad: float32 [960, 320], P('gx', 'gy')
- output_grad: float32 [960, 960], P('gx', 'gy')
- gate_grad: float32 [960, 2560], P('gx', 'gy')
- up_grad: float32 [960, 2560], P('gx', 'gy')
- down_grad: float32 [2560, 960], P('gx', 'gy')
- attgain_grad: float32 [960], replicated
- mlpgain_grad: float32 [960], replicated
Inputs may be any that keep to these rules, and one draw needn't show every extreme that they name: `segments`: segment numbers never fall along the tokens; a document may run on past the end of a sequence.
All inputs are finite; a program needn't handle non-finite values.
Results may differ from a plain program's by a relative error of at most 0.04.
Values may be sent and summed in bfloat16 or wider, within the bound.
A program may use at most 128 MiB of HBM per device.

v0:
```python
import functools

import jax
import jax.numpy as jnp
from jax import lax
from jax.experimental import pallas as pl
from jax.experimental.pallas import tpu as pltpu
from jax.sharding import PartitionSpec as P

QUERY_HEADS = 15
KEY_VALUE_HEADS = 5
GROUPS = QUERY_HEADS // KEY_VALUE_HEADS
HEAD_WIDTH = 64
SEQUENCE_LENGTH = 1024

THETA = 100000.0
EPSILON = 1e-05
MASKED = -1e30

F32 = jnp.float32
BF16 = jnp.bfloat16
MESH = pl.DeviceIdType.MESH
ANY = pl.BlockSpec(memory_space=pl.ANY)
VMEM = pl.BlockSpec(memory_space=pltpu.VMEM)


def plain_product(left, right):
    return jnp.dot(left, right, preferred_element_type=F32)


def weight_product(left, right):
    return lax.dot_general(left, right, (((0,), (0,)), ((), ())), preferred_element_type=F32)


def back_product(left, right):
    return lax.dot_general(left, right, (((1,), (1,)), ((), ())), preferred_element_type=F32)


class Net:
    def __init__(self, sizes, send_sems, recv_sems):
        self.dp, self.gx, self.gy = sizes
        self.cores = 2 if self.dp % 2 == 0 else 1
        self.hops = self.dp // self.cores
        self.d = lax.axis_index("dp")
        self.x = lax.axis_index("gx")
        self.y = lax.axis_index("gy")
        self.core = lax.rem(self.d, self.cores)
        self.hop = self.d // self.cores
        self.send_sems, self.recv_sems = send_sems, recv_sems
        self.sent, self.slots, self.pending = 0, 0, []

    def at_gx(self, j):
        return lax.rem(self.x + j, self.gx)

    def at_gy(self, k):
        return lax.rem(self.y + k, self.gy)

    def at_hop(self, i):
        return lax.rem(self.hop + i, self.hops)

    def gx_peer(self, j):
        return {"gx": self.at_gx(j)}

    def gy_peer(self, k):
        return {"gy": self.at_gy(k)}

    def hop_peer(self, i):
        return {"dp": self.at_hop(i) * self.cores + self.core}

    def core_peer(self):
        return {"dp": self.hop * self.cores + 1 - self.core}

    def dp_peer(self, i):
        return {"dp": lax.rem(self.d + i, self.dp)}

    def plane_peers(self):
        return [self.gx_peer(j) for j in range(1, self.gx)] + [
            self.gy_peer(k) for k in range(1, self.gy)
        ]

    def share_peers(self):
        peers = [self.hop_peer(i) for i in range(1, self.hops)]
        return peers + ([self.core_peer()] if self.cores == 2 else [])

    def greet(self, peers):
        barrier = pltpu.get_barrier_semaphore()
        for peer in peers:
            pl.semaphore_signal(barrier, inc=1, device_id=peer, device_id_type=MESH)
        pl.semaphore_wait(barrier, len(peers))

    def block(self, count):
        first = self.slots
        self.slots += count
        return first

    def copy(self, src, dst, slot, peer):
        return pltpu.make_async_remote_copy(
            src_ref=src,
            dst_ref=dst,
            send_sem=self.send_sems.at[self.sent],
            recv_sem=self.recv_sems.at[slot],
            device_id=peer,
            device_id_type=MESH,
        )

    def send(self, src, dst, slot, peer):
        copy = self.copy(src, dst, slot, peer)
        copy.start()
        self.sent += 1
        self.pending.append(copy)

    def arrive(self, dst, slot):
        pltpu.make_async_remote_copy(
            src_ref=dst,
            dst_ref=dst,
            send_sem=self.send_sems.at[0],
            recv_sem=self.recv_sems.at[slot],
            device_id=self.gy_peer(1),
            device_id_type=MESH,
        ).wait_recv()

    def drain(self):
        for copy in self.pending:
            copy.wait_send()


def far_first(count):
    order = list(range(1, count))
    return sorted(order, key=lambda k: -min(k, count - k))


class PlaneGather:
    def __init__(self, net, src, out):
        self.net, self.src, self.out = net, src, out
        self.gy_slot = net.block(net.gy)
        self.gx_slot = net.block(net.gx * net.gy)

    def start(self):
        net = self.net
        own = self.out(net.x, net.y)
        for k in range(1, net.gy):
            net.send(self.src, own, self.gy_slot + net.y, net.gy_peer(k))
        for j in range(1, net.gx):
            net.send(self.src, own, self.gx_slot + net.x * net.gy + net.y, net.gx_peer(j))

    def relay(self, k):
        net = self.net
        row = net.at_gy(k)
        piece = self.out(net.x, row)
        net.arrive(piece, self.gy_slot + row)
        for j in range(1, net.gx):
            net.send(piece, piece, self.gx_slot + net.x * net.gy + row, net.gx_peer(j))

    def settle(self, j, k):
        net = self.net
        side, row = net.at_gx(j), net.at_gy(k)
        net.arrive(self.out(side, row), self.gx_slot + side * net.gy + row)


class Share:
    def __init__(self, net, out):
        self.net, self.out = net, out
        self.hop_slot = net.block(net.hops)
        self.core_slot = net.block(net.dp)

    def start(self, src):
        net = self.net
        own = self.out(net.d)
        for i in range(1, net.hops):
            net.send(src, own, self.hop_slot + net.hop, net.hop_peer(i))
        if net.cores == 2:
            net.send(src, own, self.core_slot + net.d, net.core_peer())

    def relay(self):
        net = self.net
        for i in range(1, net.hops):
            hop = net.at_hop(i)
            rank = hop * net.cores + net.core
            piece = self.out(rank)
            net.arrive(piece, self.hop_slot + hop)
            if net.cores == 2:
                net.send(piece, piece, self.core_slot + rank, net.core_peer())

    def settle(self):
        net = self.net
        if net.cores == 2:
            for hop in range(net.hops):
                rank = hop * net.cores + 1 - net.core
                net.arrive(self.out(rank), self.core_slot + rank)


class PlaneSum:
    def __init__(self, net, src, landing_x, stage, landing_y):
        self.net, self.src = net, src
        self.landing_x, self.stage, self.landing_y = landing_x, stage, landing_y
        self.gx_slot = net.block(net.gx * net.gy)
        self.gy_slot = net.block(net.gy)

    def start(self, k):
        net = self.net
        row = net.at_gy(k)
        for j in range(1, net.gx):
            net.send(
                self.src(net.at_gx(j), row),
                self.landing_x.at[net.x, row],
                self.gx_slot + net.x * net.gy + row,
                net.gx_peer(j),
            )

    def relay(self, k):
        net = self.net
        row = net.at_gy(k)
        total = self.src(net.x, row)[...].astype(F32)
        for j in range(1, net.gx):
            side = net.at_gx(j)
            net.arrive(self.landing_x.at[side, row], self.gx_slot + side * net.gy + row)
            total = total + self.landing_x[side, row].astype(F32)
        if k == 0:
            self.landing_y[net.y] = total.astype(self.landing_y.dtype)
        else:
            self.stage[row] = total.astype(self.stage.dtype)
            net.send(
                self.stage.at[row], self.landing_y.at[net.y], self.gy_slot + net.y, net.gy_peer(k)
            )

    def total(self):
        net = self.net
        for k in range(1, net.gy):
            row = net.at_gy(k)
            net.arrive(self.landing_y.at[row], self.gy_slot + row)
        total = self.landing_y[0].astype(F32)
        for row in range(1, net.gy):
            total = total + self.landing_y[row].astype(F32)
        return total


def call(kernel, sizes, number, name, out_shapes, out_specs, in_specs, scratch, sends, slots):
    def body(*refs):
        net = Net(sizes, refs[-2], refs[-1])
        kernel(net, *refs[:-2])
        net.drain()
        assert net.sent <= sends and net.slots <= slots, (net.sent, net.slots)

    return pl.pallas_call(
        body,
        name=name,
        out_shape=out_shapes,
        in_specs=in_specs,
        out_specs=out_specs,
        scratch_shapes=list(scratch)
        + [pltpu.SemaphoreType.DMA((sends,)), pltpu.SemaphoreType.DMA((slots,))],
        compiler_params=pltpu.CompilerParams(collective_id=number, has_side_effects=True),
    )


def local(copies):
    for copy in copies:
        copy.start()


def wait_local(copies):
    for copy in copies:
        copy.wait()


def gather_weights(sizes, att, gate_up, down, cot, normed):
    dp, gx, gy = sizes
    hops = dp // 2
    share_count = (gx * gy + 2) * (hops - 1 + hops) + gx * gy + 2
    sends = share_count + 3 * (gx * gy) + 4
    slots = (gx * gy + 2) * (hops + dp) + 3 * (gy + gx * gy)

    def kernel(net, att_ref, gu_ref, dn_ref, cot_ref, nm_ref, att_out, gu_out, dn_out, cot_out, nm_out, sems):
        net.greet(net.plane_peers() + net.share_peers())
        att_plane = PlaneGather(net, att_ref, lambda a, b: att_out.at[a, b, net.d])
        gu_plane = PlaneGather(net, gu_ref, lambda a, b: gu_out.at[a, :, b])
        dn_plane = PlaneGather(net, dn_ref, lambda a, b: dn_out.at[a, b])
        first_hop = net.block(gx * gy * net.hops)
        first_core = net.block(gx * gy * net.dp)

        def shared(a, b):
            item = Share.__new__(Share)
            item.net = net
            item.out = lambda rank: att_out.at[a, b, rank]
            place = a * gy + b
            item.hop_slot = first_hop + place * net.hops
            item.core_slot = first_core + place * net.dp
            return item

        tokens = [(cot_ref, Share(net, lambda r: cot_out.at[r])), (nm_ref, Share(net, lambda r: nm_out.at[r]))]
        own = [
            pltpu.make_async_copy(att_ref, att_out.at[net.x, net.y, net.d], sems.at[0]),
            pltpu.make_async_copy(gu_ref, gu_out.at[net.x, :, net.y], sems.at[1]),
            pltpu.make_async_copy(dn_ref, dn_out.at[net.x, net.y], sems.at[2]),
            pltpu.make_async_copy(cot_ref, cot_out.at[net.d], sems.at[3]),
            pltpu.make_async_copy(nm_ref, nm_out.at[net.d], sems.at[4]),
        ]
        att_plane.start()
        shared(net.x, net.y).start(att_ref)
        gu_plane.start()
        dn_plane.start()
        local(own)
        for k in range(1, gy):
            att_plane.relay(k)
            row = net.at_gy(k)
            shared(net.x, row).start(att_out.at[net.x, row, net.d])
        for j in range(1, gx):
            for k in range(gy):
                att_plane.settle(j, k)
                side, row = net.at_gx(j), net.at_gy(k)
                shared(side, row).start(att_out.at[side, row, net.d])
        for ref, item in tokens:
            item.start(ref)
        for k in range(1, gy):
            gu_plane.relay(k)
            dn_plane.relay(k)
        places = [(j, k) for j in range(gx) for k in range(gy)]
        for j, k in places:
            shared(net.at_gx(j), net.at_gy(k)).relay()
        for _, item in tokens:
            item.relay()
        for j in range(1, gx):
            for k in range(gy):
                gu_plane.settle(j, k)
                dn_plane.settle(j, k)
        for j, k in places:
            shared(net.at_gx(j), net.at_gy(k)).settle()
        for _, item in tokens:
            item.settle()
        wait_local(own)

    shapes = (
        jax.ShapeDtypeStruct((gx, gy, dp) + att.shape, BF16),
        jax.ShapeDtypeStruct((gx, 2, gy) + gate_up.shape[1:], BF16),
        jax.ShapeDtypeStruct((gx, gy) + down.shape, BF16),
        jax.ShapeDtypeStruct((dp,) + cot.shape, BF16),
        jax.ShapeDtypeStruct((dp,) + normed.shape, BF16),
    )
    return call(
        kernel, sizes, 1, "gather_weights", shapes, [ANY] * 5, [VMEM] * 5,
        [pltpu.SemaphoreType.DMA((5,))], sends, slots,
    )(att, gate_up, down, cot, normed)


def turned(values):
    return jnp.transpose(values)


def head_rows(ref, first, lead=()):
    return jnp.concatenate(
        [ref[:, h * HEAD_WIDTH : (h + 1) * HEAD_WIDTH] for h in range(first, first + GROUPS)], axis=0
    )


def key_columns(ref, place):
    columns = ref[:, :, :, place * HEAD_WIDTH : (place + 1) * HEAD_WIDTH]
    return columns.reshape(-1, HEAD_WIDTH)


def put_heads(ref, first, rows, values):
    for n in range(GROUPS):
        lanes = slice((first + n) * HEAD_WIDTH, (first + n + 1) * HEAD_WIDTH)
        ref[:, lanes] = values[n * rows : (n + 1) * rows].astype(ref.dtype)


def attend_heads(q_ref, kv_ref, bias_ref, mixed_ref, logsum_ref):
    rows = q_ref.shape[0]
    bias = jnp.concatenate([bias_ref[...]] * GROUPS, axis=1)
    for k in range(KEY_VALUE_HEADS):
        query = head_rows(q_ref, k * GROUPS)
        scores = back_product(key_columns(kv_ref, k), query) * HEAD_WIDTH ** (-0.5) + bias
        highest = jnp.max(scores, axis=0, keepdims=True)
        weights = jnp.exp(scores - highest)
        sums = jnp.sum(weights, axis=0, keepdims=True)
        logsum_ref[k : k + 1, :] = highest + jnp.log(sums)
        probs = (weights * (1.0 / sums)).astype(BF16)
        mixed = weight_product(key_columns(kv_ref, KEY_VALUE_HEADS + k), probs)
        put_heads(mixed_ref, k * GROUPS, rows, turned(mixed))


def attend_heads_back(q_ref, kv_ref, bias_ref, logsum_ref, mixed_ref, dmixed_ref, dq_ref, dkv_ref):
    rows = q_ref.shape[0]
    bias = jnp.concatenate([bias_ref[...]] * GROUPS, axis=1)
    blocks = kv_ref.shape[:3]
    for k in range(KEY_VALUE_HEADS):
        query = head_rows(q_ref, k * GROUPS)
        mixed = head_rows(mixed_ref, k * GROUPS)
        dmixed = head_rows(dmixed_ref, k * GROUPS)
        keys = key_columns(kv_ref, k)
        scores = back_product(keys, query) * HEAD_WIDTH ** (-0.5) + bias
        weights = jnp.exp(scores - logsum_ref[k : k + 1, :])
        delta = jnp.sum(turned(mixed.astype(F32) * dmixed.astype(F32)), axis=0, keepdims=True)
        dprobs = back_product(key_columns(kv_ref, KEY_VALUE_HEADS + k), dmixed)
        dscores = (weights * (dprobs - delta)).astype(BF16)
        dquery = weight_product(keys, dscores) * HEAD_WIDTH ** (-0.5)
        put_heads(dq_ref, k * GROUPS, rows, turned(dquery))
        dkeys = plain_product(dscores, query) * HEAD_WIDTH ** (-0.5)
        dvalues = plain_product(weights.astype(BF16), dmixed)
        lanes = slice(k * HEAD_WIDTH, (k + 1) * HEAD_WIDTH)
        dkv_ref[:, :, :, lanes] = dkeys.astype(BF16).reshape(blocks + (HEAD_WIDTH,))
        place = KEY_VALUE_HEADS + k
        lanes = slice(place * HEAD_WIDTH, (place + 1) * HEAD_WIDTH)
        dkv_ref[:, :, :, lanes] = dvalues.astype(BF16).reshape(blocks + (HEAD_WIDTH,))


def attend(sizes, query, piece, bias):
    dp, gx, gy = sizes

    def kernel(net, q_ref, src, bias_ref, out, mixed_ref, logsum_ref, sems):
        net.greet(net.plane_peers())
        plane = PlaneGather(net, src, lambda a, b: out.at[a, b])
        own = [pltpu.make_async_copy(src, out.at[net.x, net.y], sems.at[0])]
        plane.start()
        local(own)
        for k in range(1, gy):
            plane.relay(k)
        for j in range(1, gx):
            for k in range(gy):
                plane.settle(j, k)
        wait_local(own)
        attend_heads(q_ref, out, bias_ref, mixed_ref, logsum_ref)

    rows = query.shape[0]
    shapes = (
        jax.ShapeDtypeStruct((gx, gy) + piece.shape, piece.dtype),
        jax.ShapeDtypeStruct(query.shape, BF16),
        jax.ShapeDtypeStruct((KEY_VALUE_HEADS, GROUPS * rows), F32),
    )
    return call(
        kernel, sizes, 2, "attend", shapes, [VMEM] * 3, [VMEM] * 3,
        [pltpu.SemaphoreType.DMA((1,))], gx * gy + gy, gy + gx * gy,
    )(query, piece, bias)


def attend_back(query, kv_all, bias, logsum, mixed, dmixed):
    return pl.pallas_call(
        attend_heads_back,
        name="attend_back",
        out_shape=(
            jax.ShapeDtypeStruct(query.shape, F32),
            jax.ShapeDtypeStruct(kv_all.shape, BF16),
        ),
        in_specs=[VMEM] * 6,
        out_specs=[VMEM] * 2,
    )(query, kv_all, bias, logsum, mixed, dmixed)


def mlp(normed_all, cot_all, gate_up, down):
    gx, both, fan = gate_up.shape
    rows, width = normed_all.shape
    hidden = both // 2
    part = down.shape[2]
    step = rows // 2 if rows % 32 == 0 else rows

    def kernel(n_ref, c_ref, gu_ref, dt_ref, dn_ref, mo_ref, gg_ref, dg_ref, act_ref, delta_ref):
        def tokens(i, carry):
            span = pl.ds(pl.multiple_of(i * step, step), step)
            normed, cot = n_ref[span, :], c_ref[span, :]
            gate_up_rows = sum(
                back_product(normed[:, a * fan : (a + 1) * fan], gu_ref[a]) for a in range(gx)
            ).astype(BF16)
            gate = gate_up_rows[:, :hidden].astype(F32)
            up = gate_up_rows[:, hidden:].astype(F32)
            dact = jnp.concatenate([plain_product(cot, dt_ref[a]) for a in range(gx)], axis=1)
            sigmoid = jax.nn.sigmoid(gate)
            act = (gate * sigmoid * up).astype(BF16)
            gate_delta = (dact * up * sigmoid * (1.0 + gate * (1.0 - sigmoid))).astype(BF16)
            up_delta = (dact * gate * sigmoid).astype(BF16)
            deltas = jnp.concatenate([gate_delta, up_delta], axis=1)
            delta_ref[span, :] = deltas
            for a in range(gx):
                act_ref[a, span, :] = act[:, a * part : (a + 1) * part]
                dn_ref[span, a * fan : (a + 1) * fan] = plain_product(deltas, gu_ref[a]).astype(BF16)
            mo_ref[span, :] = sum(
                back_product(act[:, a * part : (a + 1) * part], dt_ref[a]) for a in range(gx)
            ).astype(BF16)
            return carry

        lax.fori_loop(0, rows // step, tokens, 0)
        for a in range(gx):
            gg_ref[a] = weight_product(delta_ref[...], n_ref[:, a * fan : (a + 1) * fan]).astype(BF16)
            dg_ref[a] = weight_product(c_ref[...], act_ref[a]).astype(BF16)

    return pl.pallas_call(
        kernel,
        name="mlp",
        out_shape=(
            jax.ShapeDtypeStruct(normed_all.shape, BF16),
            jax.ShapeDtypeStruct(normed_all.shape, BF16),
            jax.ShapeDtypeStruct(gate_up.shape, BF16),
            jax.ShapeDtypeStruct(down.shape, BF16),
        ),
        in_specs=[VMEM] * 4,
        out_specs=[VMEM] * 4,
        scratch_shapes=[pltpu.VMEM((gx, rows, part), BF16), pltpu.VMEM((rows, both), BF16)],
    )(normed_all, cot_all, gate_up, down)


def share_tokens(sizes, *pieces):
    dp, gx, gy = sizes
    count = len(pieces)

    def kernel(net, *refs):
        srcs, outs, sems = refs[:count], refs[count : 2 * count], refs[2 * count]
        net.greet(net.share_peers())
        items = [Share(net, lambda r, out=out: out.at[r]) for out in outs]
        own = [
            pltpu.make_async_copy(src, out.at[net.d], sems.at[n])
            for n, (src, out) in enumerate(zip(srcs, outs))
        ]
        for item, src in zip(items, srcs):
            item.start(src)
        local(own)
        for item in items:
            item.relay()
        for item in items:
            item.settle()
        wait_local(own)

    shapes = tuple(jax.ShapeDtypeStruct((dp,) + p.shape, p.dtype) for p in pieces)
    return call(
        kernel, sizes, 3, "share_tokens", shapes, [ANY] * count, [VMEM] * count,
        [pltpu.SemaphoreType.DMA((count,))], count * dp, count * (dp // 2 + dp),
    )(*pieces)


def sum_tokens(sizes, *parts):
    dp, gx, gy = sizes
    count = len(parts)
    hops = dp // 2
    shape = parts[0].shape[1:]

    def kernel(net, *refs):
        srcs, outs, scratch = refs[:count], refs[count : 2 * count], refs[2 * count :]
        landing_core, stage, landing_hop = scratch[:count], scratch[count : 2 * count], scratch[2 * count :]
        net.greet(net.share_peers())
        core_slots = [net.block(net.hops) for _ in range(count)]
        hop_slots = [net.block(net.hops) for _ in range(count)]
        order = list(range(1, net.hops)) + [0]
        for n in range(count):
            for i in order:
                hop = net.at_hop(i)
                net.send(
                    srcs[n].at[hop * 2 + 1 - net.core], landing_core[n].at[hop],
                    core_slots[n] + hop, net.core_peer(),
                )
        for n in range(count):
            for i in order:
                hop = net.at_hop(i)
                net.arrive(landing_core[n].at[hop], core_slots[n] + hop)
                total = srcs[n][hop * 2 + net.core].astype(F32) + landing_core[n][hop].astype(F32)
                if i == 0:
                    outs[n][...] = total
                else:
                    stage[n][hop] = total.astype(BF16)
                    net.send(
                        stage[n].at[hop], landing_hop[n].at[net.hop],
                        hop_slots[n] + net.hop, net.hop_peer(i),
                    )
        for n in range(count):
            for i in range(1, net.hops):
                hop = net.at_hop(i)
                net.arrive(landing_hop[n].at[hop], hop_slots[n] + hop)
                outs[n][...] += landing_hop[n][hop].astype(F32)

    shapes = tuple(jax.ShapeDtypeStruct(shape, F32) for _ in parts)
    slab = pltpu.VMEM((hops,) + shape, BF16)
    return call(
        kernel, sizes, 4, "sum_tokens", shapes, [VMEM] * count, [VMEM] * count,
        [slab] * (3 * count), count * dp, count * dp,
    )(*parts)


def sum_plane(sizes, blocks):
    dp, gx, gy = sizes
    shape = blocks.shape[2:]

    def kernel(net, src, out, landing_x, stage, landing_y):
        net.greet(net.plane_peers())
        item = PlaneSum(net, lambda a, b: src.at[a, b], landing_x, stage, landing_y)
        order = far_first(gy) + [0]
        for k in order:
            item.start(k)
        for k in order:
            item.relay(k)
        out[...] = item.total()

    slab = pltpu.VMEM((gy,) + shape, BF16)
    return call(
        kernel, sizes, 5, "sum_plane", jax.ShapeDtypeStruct(shape, F32), VMEM, [VMEM],
        [pltpu.VMEM((gx, gy) + shape, BF16), slab, slab], gx * gy + gy, gx * gy + gy,
    )(blocks)


def trade_tokens(sizes, blocks):
    dp, gx, gy = sizes

    def kernel(net, src, out, sems):
        peers = [net.dp_peer(i) for i in range(1, dp)]
        net.greet(peers)
        slot = net.block(dp)
        for i in range(1, dp):
            rank = lax.rem(net.d + i, dp)
            net.send(src.at[rank], out.at[net.d], slot + net.d, net.dp_peer(i))
        own = pltpu.make_async_copy(src.at[net.d], out.at[net.d], sems.at[0])
        own.start()
        for i in range(1, dp):
            rank = lax.rem(net.d + i, dp)
            net.arrive(out.at[rank], slot + rank)
        own.wait()

    return call(
        kernel, sizes, 6, "trade_tokens", jax.ShapeDtypeStruct(blocks.shape, blocks.dtype), ANY, [VMEM],
        [pltpu.SemaphoreType.DMA((1,))], dp, dp,
    )(blocks)


def reduce_weights(sizes, gate_up, down, att, gains):
    dp, gx, gy = sizes
    halves = gate_up.shape[1]
    pieces = [gate_up.shape[3:]] * halves + [down.shape[2:], att.shape[2:]]
    count = len(pieces)

    def kernel(net, gu_ref, dn_ref, att_ref, gain_ref, *refs):
        gu_out, dn_out, att_out, gain_out = refs[:4]
        refs = refs[4:]
        landing_x, stage, landing_y, result = (refs[n * (count + 1) : (n + 1) * (count + 1)] for n in range(4))
        sems = refs[-1]
        net.greet(net.plane_peers() + net.share_peers())
        sources = [lambda a, b, n=n: gu_ref.at[a, n, b] for n in range(halves)]
        sources += [lambda a, b: dn_ref.at[a, b], lambda a, b: att_ref.at[a, b], lambda a, b: gain_ref]
        outs = [lambda r, n=n: gu_out.at[r, n] for n in range(halves)]
        outs += [lambda r: dn_out.at[r], lambda r: att_out.at[r], lambda r: gain_out.at[r]]
        sums = [
            PlaneSum(net, sources[n], landing_x[n], stage[n], landing_y[n]) for n in range(count + 1)
        ]
        shares = [Share(net, out) for out in outs]
        order = far_first(gy) + [0]
        for k in order:
            for item in sums:
                item.start(k)
        for k in order:
            for item in sums:
                item.relay(k)
        own = []
        for n, (item, share) in enumerate(zip(sums, shares)):
            result[n][...] = item.total().astype(result[n].dtype)
            share.start(result[n])
            own.append(pltpu.make_async_copy(result[n], share.out(net.d), sems.at[n]))
            own[-1].start()
        for share in shares:
            share.relay()
        for share in shares:
            share.settle()
        wait_local(own)

    shapes = (
        jax.ShapeDtypeStruct((dp, halves) + pieces[0], BF16),
        jax.ShapeDtypeStruct((dp,) + pieces[-2], BF16),
        jax.ShapeDtypeStruct((dp,) + pieces[-1], BF16),
        jax.ShapeDtypeStruct((dp,) + gains.shape, F32),
    )
    kinds = [(piece, BF16) for piece in pieces] + [(gains.shape, F32)]
    scratch = [pltpu.VMEM((gx, gy) + p, t) for p, t in kinds]
    scratch += [pltpu.VMEM((gy,) + p, t) for p, t in kinds] * 2
    scratch += [pltpu.VMEM(p, t) for p, t in kinds]
    scratch += [pltpu.SemaphoreType.DMA((count + 1,))]
    return call(
        kernel, sizes, 7, "reduce_weights", shapes, [ANY] * 4, [VMEM] * 4, scratch,
        (count + 1) * (gx * gy + gy + dp), (count + 1) * (gx * gy + gy + dp + dp // 2),
    )(gate_up, down, att, gains)


def rope_angles(positions):
    half_dim = HEAD_WIDTH // 2
    inverse = THETA ** (-(jnp.arange(half_dim, dtype=F32) * 2.0 / HEAD_WIDTH))
    angles = positions[:, None] * inverse[None, :]
    return (jnp.cos(angles)[:, None, :], jnp.sin(angles)[:, None, :])


def rotate(values, cos_table, sin_table):
    item_count = values.shape[0]
    shaped = values.reshape(item_count, -1, HEAD_WIDTH)
    half_dim = HEAD_WIDTH // 2
    front_part = shaped[:, :, :half_dim]
    back_part = shaped[:, :, half_dim:]
    turned = jnp.concatenate(
        [
            front_part * cos_table - back_part * sin_table,
            back_part * cos_table + front_part * sin_table,
        ],
        axis=2,
    )
    return turned.reshape(item_count, -1)


def unrotate(values, cos_table, sin_table):
    return rotate(values, cos_table, -sin_table)


def normalize(values, gain):
    rms_rows = lax.rsqrt(jnp.mean(values * values, axis=1, keepdims=True) + EPSILON)
    unit_rows = values * rms_rows
    return (rms_rows, unit_rows, (unit_rows * gain).astype(BF16))


def normalize_back(dnormed, gain, rms_rows, unit_rows):
    scaled = dnormed * gain
    dvalues = rms_rows * (scaled - unit_rows * jnp.mean(scaled * unit_rows, axis=1, keepdims=True))
    return (dvalues, jnp.sum(dnormed * unit_rows, axis=0))


def on_device(
    sizes,
    inputs,
    segments,
    attn_gain,
    query_weight,
    key_weight,
    value_weight,
    output_weight,
    mlp_gain,
    gate_weight,
    up_weight,
    down_weight,
    cotangent,
):
    dp, gx, gy = sizes
    count_of_rows, width = inputs.shape
    rank = lax.axis_index("dp")
    begin_row = (lax.axis_index("gx") * gy + lax.axis_index("gy")) * count_of_rows
    seq_begin = begin_row // SEQUENCE_LENGTH * SEQUENCE_LENGTH
    local_places = begin_row - seq_begin + jnp.arange(count_of_rows)
    cos_table, sin_table = rope_angles(local_places.astype(F32))
    query_segs = lax.dynamic_slice_in_dim(segments, begin_row, count_of_rows, 0)
    allowed = (jnp.arange(SEQUENCE_LENGTH)[:, None] <= local_places[None, :]) & (
        query_segs[None, :] == segments[:, None]
    )
    bias = jnp.where(allowed, 0.0, MASKED).astype(F32)
    residual = inputs.astype(F32)
    rms_one, unit_one, normed_one = normalize(residual, attn_gain)

    fan = query_weight.shape[0]
    q_cols, k_cols, v_cols = query_weight.shape[1], key_weight.shape[1], value_weight.shape[1]
    o_cols = output_weight.shape[1]
    qkv_cols = q_cols + k_cols + v_cols
    all_cols = qkv_cols + o_cols
    att_share = all_cols // dp
    packed = jnp.concatenate([query_weight, key_weight, value_weight, output_weight], axis=1).T
    att_part = lax.dynamic_slice_in_dim(packed, rank * att_share, att_share, 0)
    share = gate_weight.shape[1] // dp
    groups = gy // gx
    gate_up_part = jnp.stack(
        [
            lax.dynamic_slice_in_dim(gate_weight, rank * share, share, 1).T,
            lax.dynamic_slice_in_dim(up_weight, rank * share, share, 1).T,
        ]
    )
    down_cols = down_weight.shape[1]
    down_part = lax.dynamic_slice_in_dim(
        down_weight.reshape(groups, dp, share, down_cols), rank, 1, 1
    ).reshape(groups * share, down_cols).T

    att_all, gate_up_all, down_all, cot_all, normed_one_all = gather_weights(
        sizes, att_part, gate_up_part, down_part, cotangent, normed_one
    )
    att_all = att_all.reshape(gx, gy, all_cols, fan)
    qkv_rows = att_all[:, :, :qkv_cols].reshape(gx, gy * qkv_cols, fan)
    out_rows = att_all[:, :, qkv_cols:].reshape(gx, gy * o_cols, fan)
    hidden_width = gy * share
    gate_up_all = gate_up_all.reshape(gx, 2 * hidden_width, fan)
    half_hidden = groups * share
    down_all = down_all.reshape(gx, gy * down_cols, half_hidden)
    cot_all = cot_all.reshape(dp * count_of_rows, width)
    normed_one_all = normed_one_all.reshape(dp * count_of_rows, width)

    def parts(rows):
        return [rows[:, a * fan : (a + 1) * fan] for a in range(gx)]

    def onto(rows, weights):
        return sum(back_product(part, weights[a]) for a, part in enumerate(parts(rows)))

    def back_onto(rows, weights):
        return jnp.concatenate([plain_product(rows, weights[a]) for a in range(gx)], axis=1)

    qkv = onto(normed_one, qkv_rows).astype(BF16).reshape(count_of_rows, gy, qkv_cols)
    query_rows = qkv[:, :, :q_cols].reshape(count_of_rows, -1)
    key_rows = qkv[:, :, q_cols : q_cols + k_cols].reshape(count_of_rows, -1)
    value_rows = qkv[:, :, q_cols + k_cols :].reshape(count_of_rows, -1)
    rotated_query = rotate(query_rows.astype(F32), cos_table, sin_table).astype(BF16)
    rotated_key = rotate(key_rows.astype(F32), cos_table, sin_table).astype(BF16)
    kv_width = rotated_key.shape[1]
    kv_all, attention_mixture, logsum = attend(
        sizes, rotated_query, jnp.concatenate([rotated_key, value_rows], axis=1), bias
    )
    attn_out = lax.optimization_barrier(onto(attention_mixture, out_rows).astype(BF16))
    hidden = residual + attn_out.astype(F32)
    rms_two, unit_two, normed_two = normalize(hidden, mlp_gain)

    normed_all, mixed_all = share_tokens(sizes, normed_two, attention_mixture)
    normed_all = normed_all.reshape(dp * count_of_rows, width)
    mixed_all = mixed_all.reshape(dp * count_of_rows, width)
    dnormed_part, mlp_part, gate_up_grad, down_grad = mlp(normed_all, cot_all, gate_up_all, down_all)
    dnormed_two, mlp_out = sum_tokens(
        sizes,
        dnormed_part.reshape(dp, count_of_rows, width),
        mlp_part.reshape(dp, count_of_rows, width),
    )
    layer_out = (hidden + mlp_out).astype(BF16)

    gate_up_grad = gate_up_grad.reshape(gx, 2, gy, share, fan)
    down_grad = down_grad.reshape(gx, gy, down_cols, half_hidden)

    dhidden_norm, mlpgain_part = normalize_back(dnormed_two, mlp_gain, rms_two, unit_two)
    dhidden = cotangent.astype(F32) + dhidden_norm
    dhidden_bf = dhidden.astype(BF16)
    mixture_gradient = back_onto(dhidden_bf, out_rows).astype(BF16)
    dquery_rot, dkv = attend_back(
        rotated_query, kv_all, bias, logsum, attention_mixture, mixture_gradient
    )
    dkv = sum_plane(sizes, dkv)
    dquery = unrotate(dquery_rot, cos_table, sin_table).astype(BF16)
    dkey = unrotate(dkv[:, :kv_width], cos_table, sin_table).astype(BF16)
    dvalue_bf = dkv[:, kv_width:].astype(BF16)
    dqkv = jnp.concatenate(
        [
            dquery.reshape(count_of_rows, gy, q_cols),
            dkey.reshape(count_of_rows, gy, k_cols),
            dvalue_bf.reshape(count_of_rows, gy, v_cols),
        ],
        axis=2,
    )
    dall = jnp.concatenate([dqkv, dhidden_bf.reshape(count_of_rows, gy, o_cols)], axis=2)
    dall = dall.reshape(count_of_rows, gy, dp, att_share).transpose(2, 0, 1, 3)
    dall = trade_tokens(sizes, dall.reshape(dp, count_of_rows, gy * att_share))
    dall = dall.reshape(dp * count_of_rows, gy * att_share)
    places = rank * att_share + lax.broadcasted_iota(jnp.int32, (gy, att_share, 1), 1)
    from_normed = (places < qkv_cols).reshape(gy * att_share, 1)
    att_grad = jnp.stack(
        [
            jnp.where(from_normed, weight_product(dall, one), weight_product(dall, two)).astype(BF16)
            for one, two in zip(parts(normed_one_all), parts(mixed_all))
        ]
    ).reshape(gx, gy, att_share, fan)
    dnormed_one = back_onto(dqkv.reshape(count_of_rows, gy * qkv_cols), qkv_rows)
    dresidual, attgain_part = normalize_back(dnormed_one, attn_gain, rms_one, unit_one)
    input_grad = (dhidden + dresidual).astype(BF16)
    gain_parts = jnp.concatenate([attgain_part, mlpgain_part])
    gain_rows = -(-gain_parts.shape[0] // 1024) * 8
    gain_parts = jnp.pad(gain_parts, (0, gain_rows * 128 - gain_parts.shape[0])).reshape(gain_rows, 128)

    gate_up_sum, down_sum, att_sum, gain_sum = reduce_weights(
        sizes, gate_up_grad, down_grad, att_grad, gain_parts
    )
    gate_grad = gate_up_sum[:, 0].reshape(dp * share, fan).T.astype(F32)
    up_grad = gate_up_sum[:, 1].reshape(dp * share, fan).T.astype(F32)
    down_grad = (
        down_sum.reshape(dp, down_cols, groups, share)
        .transpose(2, 0, 3, 1)
        .reshape(down_weight.shape)
        .astype(F32)
    )
    att_sum = att_sum.reshape(all_cols, fan).T.astype(F32)
    gains = jnp.sum(gain_sum, axis=0).reshape(-1)
    return (
        layer_out,
        input_grad,
        att_sum[:, :q_cols],
        att_sum[:, q_cols : q_cols + k_cols],
        att_sum[:, q_cols + k_cols : qkv_cols],
        att_sum[:, qkv_cols:],
        gate_grad,
        up_grad,
        down_grad,
        gains[:width],
        gains[width : 2 * width],
    )


def solution(mesh):
    sizes = (mesh.shape["dp"], mesh.shape["gx"], mesh.shape["gy"])
    tokens = P(("dp", "gx", "gy"), None)
    block = P("gx", "gy")
    return jax.shard_map(
        functools.partial(on_device, sizes),
        mesh=mesh,
        in_specs=(tokens, P("dp"), P(), block, block, block, block, P(), block, block, block, tokens),
        out_specs=(tokens, tokens) + (block,) * 7 + (P(), P()),
        check_vma=False,
    )
```

profile of v0, /device:TPU:31, one launch (start us, length us, event | category | flops | bytes accessed | tf_op | source)
XLA Modules:
  0.0 391.2 jit_solution(9738966633276889785)
XLA Ops:
  11.0 78.3 %gather_weights.1 = (bf16[2,4,4,160,480]{4,3,2,1,0:T(8,128)(2,1)}, bf16[2,2,4,160,480]{4,3,2,1,0:T(8,128)(2,1)}, bf16[2,4,240,320]{3,2,1,0:T(8,128)(2,1)}, bf16[...) custom-call(bf16[160,480]{1,0:T(8,128)(2,1)} %fusion.27.refs_0_, bf16[2,160,480]{2,1,0:T(8,128)(2,1)} %pad_maximum_fusion.4.refs_1_, ...), custom_call_target="tpu_custom_call" | custom-call | tf_op jit(solution)/shard_map/gather_weights/pallas_call | solution.py:339
  89.4 2.3 fusion.39
  98.8 1.8 copy.97.refs_0_.q_ref
  107.8 1.7 pad_maximum_fusion.8.refs_1_
  110.2 1.7 fusion.22.refs_2_.bias_ref
  112.0 43.0 %attend.1 = (bf16[2,4,128,640]{3,2,1,0:T(8,128)(2,1)}, bf16[128,960]{1,0:T(8,128)(2,1)}, f32[5,384]{1,0:T(8,128)}) custom-call(bf16[128,960]{1,0:T(8,128)(2,1)} %copy.97.refs_0_.q_ref, bf16[128,640]{1,0:T(8,128)(2,1)} %pad_maximum_fusion.8.refs_1_, f32[1024,128]{1,0:T(8,128)} %fusion.22.refs_2_.bias_ref), custom_call_target="tpu_custom_call" | custom-call | tf_op jit(solution)/shard_map/attend/pallas_call | solution.py:429
  155.0 1.7 fusion.38
  159.3 1.8 copy.98
  162.7 1.8 multiply_convert_fusion.refs_0_
  164.5 17.0 %share_tokens.1 = (bf16[4,128,960]{2,1,0:T(8,128)(2,1)}, bf16[4,128,960]{2,1,0:T(8,128)(2,1)}) custom-call(bf16[128,960]{1,0:T(8,128)(2,1)} %multiply_convert_fusion.refs_0_, bf16[128,960]{1,0:T(8,128)(2,1)} %get-tuple-element.34.refs_1_.mixed_ref), custom_call_target="tpu_custom_call" | custom-call | tf_op jit(solution)/shard_map/share_tokens/pallas_call | solution.py:521
  181.6 12.7 %mlp.1 = (bf16[512,960]{1,0:T(8,128)(2,1)}, bf16[512,960]{1,0:T(8,128)(2,1)}, bf16[2,1280,480]{2,1,0:T(8,128)(2,1)}, bf16[2,960,320]{2,1,0:T(8,128)(2,1)}) custom-call(bf16[512,960]{1,0:T(8,128)(2,1)} %bitcast.119, bf16[512,960]{1,0:T(8,128)(2,1)} %bitcast.118, bf16[2,1280,480]{2,1,0:T(8,128)(2,1)} %bitcast.103, bf16[2,960,320]{2,1,0:T(8,128)(2,1)} %bitcast.112), custom_call_target="tpu_custom_call" | custom-call | tf_op jit(solution)/shard_map/mlp/pallas_call | solution.py:484
  194.3 18.6 %sum_tokens.1 = (f32[128,960]{1,0:T(8,128)}, f32[128,960]{1,0:T(8,128)}) custom-call(bf16[4,128,960]{2,1,0:T(8,128)(2,1)} %bitcast.116, bf16[4,128,960]{2,1,0:T(8,128)(2,1)} %bitcast.117), custom_call_target="tpu_custom_call" | custom-call | tf_op jit(solution)/shard_map/sum_tokens/pallas_call | solution.py:568
  212.9 2.1 multiply_reduce_fusion
  219.9 2.5 convolution_convert_fusion.1
  224.0 1.8 pad_maximum_fusion.5.dmixed_ref
  225.8 8.5 %attend_back.1 = (f32[128,960]{1,0:T(8,128)}, bf16[2,4,128,640]{3,2,1,0:T(8,128)(2,1)}) custom-call(bf16[128,960]{1,0:T(8,128)(2,1)} %copy.97.refs_0_.q_ref, bf16[2,4,128,640]{3,2,1,0:T(8,128)(2,1)} %get-tuple-element.43.kv_ref, f32[1024,128]{1,0:T(8,128)} %fusion.22.refs_2_.bias_ref, f32[5,384]{1,0:T(8,128)} %get-tuple-element.44.logsum_ref, ...), custom_call_target="tpu_custom_call" | custom-call | tf_op jit(solution)/shard_map/attend_back/pallas_call | solution.py:436
  234.2 21.5 %sum_plane.1 = f32[128,640]{1,0:T(8,128)} custom-call(bf16[2,4,128,640]{3,2,1,0:T(8,128)(2,1)} %get-tuple-element.46.refs_0_), custom_call_target="tpu_custom_call" | custom-call | tf_op jit(solution)/shard_map/sum_plane/pallas_call | solution.py:589
  255.8 1.7 slice.208
  260.7 1.7 copy.104
  264.0 2.0 copy.103
  272.9 13.6 %trade_tokens.1 = bf16[4,128,640]{2,1,0:T(8,128)(2,1)} custom-call(bf16[4,128,640]{2,1,0:T(8,128)(2,1)} %copy.110.refs_0_), custom_call_target="tpu_custom_call" | custom-call | tf_op jit(solution)/shard_map/trade_tokens/pallas_call | solution.py:612
  286.6 2.1 fusion.16
  288.7 2.0 fusion.2
  295.1 85.7 %reduce_weights.1 = (bf16[4,2,160,480]{3,2,1,0:T(8,128)(2,1)}, bf16[4,240,320]{2,1,0:T(8,128)(2,1)}, bf16[4,160,480]{2,1,0:T(8,128)(2,1)}, f32[4,16,128]{2,1,0:T(8,128)}) custom-call(bf16[2,2,4,160,480]{4,3,2,1,0:T(8,128)(2,1)} %bitcast.104, bf16[2,4,240,320]{3,2,1,0:T(8,128)(2,1)} %bitcast.113, bf16[2,4,160,480]{3,2,1,0:T(8,128)(2,1)} %pad_maximum_fusion.refs_2_, ...), custom_call_target="tpu_custom_call" | custom-call | tf_op jit(solution)/shard_map/reduce_weights/pallas_call | solution.py:668
  (163 shorter events, 62.3 us)
Async XLA Ops:
  0.6 3.3 copy-start.25
  0.7 3.3 copy-start.26
  5.1 2.4 copy-start.21
  6.7 1.9 copy-start.23
  7.5 2.7 copy-start.28
  89.4 2.3 copy-start.10
  97.0 1.9 copy-start.24
  155.0 2.7 copy-start.9
  156.7 1.4 copy-start.1
  212.9 2.1 copy-start.4
  212.9 4.2 %copy-start.2 = (bf16[1,4,240,480]{3,2,1,0:T(8,128)(2,1)S(1)}, bf16[1,4,240,480]{3,2,1,0:T(8,128)(2,1)}, u32[]{:S(2)}) copy-start(bf16[1,4,240,480]{3,2,1,0:T(8,128)(2,1)} %copy-done.1) | copy-start | bytes 2764804
  267.9 1.4 copy-start.22
  267.9 1.4 copy-start.27
  268.0 1.3 copy-start.33
  268.0 1.3 copy-start.37
  269.3 2.2 copy-start.8
  269.8 1.9 copy-start.12
  269.8 1.9 copy-start.16
  269.8 1.9 copy-start.18
  271.8 14.7 %copy-start.38 = (bf16[4,128,960]{2,1,0:T(8,128)(2,1)S(1)}, bf16[4,128,960]{2,1,0:T(8,128)(2,1)}, u32[]{:S(2)}) copy-start(bf16[4,128,960]{2,1,0:T(8,128)(2,1)} %get-tuple-element.49) | copy-start | bytes 2949124
  286.5 2.2 copy-start.20
  383.5 1.8 copy-start.14
  387.3 1.4 copy-start.19
  389.1 1.4 copy-start.30
  (16 other events, 15.6 us)
where the time goes:
time: 397 us; the launch traced here: 391 us
  Pallas kernels  299 us (75%)
  local copies, waits for them, and re-layouts  48.9 us (12%)
  other arithmetic  29.3 us (7%)
  matrix products  12.6 us (3%)
    pallas_call x1, Pallas kernels, reduce_weights(): call(kernel, sizes, 7, 'reduce_weights', shapes, [ANY] * 4, [VMEM] * 4, s...  85.7 us
    pallas_call x1, Pallas kernels, gather_weights(): call(kernel, sizes, 1, 'gather_weights', shapes, [ANY] * 5, [VMEM] * 5, [...  78.3 us
    pallas_call x1, Pallas kernels, attend(): call(kernel, sizes, 2, 'attend', shapes, [VMEM] * 3, [VMEM] * 3, [pltpu.S...  43 us
    pallas_call x1, Pallas kernels, sum_plane(): call(kernel, sizes, 5, 'sum_plane', jax.ShapeDtypeStruct(shape, F32), VME...  21.5 us
    pallas_call x1, Pallas kernels, sum_tokens(): call(kernel, sizes, 4, 'sum_tokens', shapes, [VMEM] * count, [VMEM] * cou...  18.6 us
    pallas_call x1, Pallas kernels, share_tokens(): call(kernel, sizes, 3, 'share_tokens', shapes, [ANY] * count, [VMEM] * co...  17 us
    unnamed x92, local copies, waits for them, and re-layouts  14 us
    pallas_call x1, Pallas kernels, trade_tokens(): call(kernel, sizes, 6, 'trade_tokens', jax.ShapeDtypeStruct(blocks.shape,...  13.6 us

commit v1 on v0

--- a/solution.py
+++ b/solution.py
@@ -136,10 +136,18 @@
         self.gx_slot = net.block(net.gx * net.gy)
 
     def start(self):
+        self.start_gy()
+        self.start_gx()
+
+    def start_gy(self):
         net = self.net
         own = self.out(net.x, net.y)
         for k in range(1, net.gy):
             net.send(self.src, own, self.gy_slot + net.y, net.gy_peer(k))
+
+    def start_gx(self):
+        net = self.net
+        own = self.out(net.x, net.y)
         for j in range(1, net.gx):
             net.send(self.src, own, self.gx_slot + net.x * net.gy + net.y, net.gx_peer(j))
 
@@ -263,18 +271,13 @@
         copy.wait()
 
 
-def gather_weights(sizes, att, gate_up, down, cot, normed):
+def gather_weights(sizes, att):
     dp, gx, gy = sizes
     hops = dp // 2
-    share_count = (gx * gy + 2) * (hops - 1 + hops) + gx * gy + 2
-    sends = share_count + 3 * (gx * gy) + 4
-    slots = (gx * gy + 2) * (hops + dp) + 3 * (gy + gx * gy)
-
-    def kernel(net, att_ref, gu_ref, dn_ref, cot_ref, nm_ref, att_out, gu_out, dn_out, cot_out, nm_out, sems):
+
+    def kernel(net, att_ref, att_out, sems):
         net.greet(net.plane_peers() + net.share_peers())
         att_plane = PlaneGather(net, att_ref, lambda a, b: att_out.at[a, b, net.d])
-        gu_plane = PlaneGather(net, gu_ref, lambda a, b: gu_out.at[a, :, b])
-        dn_plane = PlaneGather(net, dn_ref, lambda a, b: dn_out.at[a, b])
         first_hop = net.block(gx * gy * net.hops)
         first_core = net.block(gx * gy * net.dp)
 
@@ -287,18 +290,9 @@
             item.core_slot = first_core + place * net.dp
             return item
 
-        tokens = [(cot_ref, Share(net, lambda r: cot_out.at[r])), (nm_ref, Share(net, lambda r: nm_out.at[r]))]
-        own = [
-            pltpu.make_async_copy(att_ref, att_out.at[net.x, net.y, net.d], sems.at[0]),
-            pltpu.make_async_copy(gu_ref, gu_out.at[net.x, :, net.y], sems.at[1]),
-            pltpu.make_async_copy(dn_ref, dn_out.at[net.x, net.y], sems.at[2]),
-            pltpu.make_async_copy(cot_ref, cot_out.at[net.d], sems.at[3]),
-            pltpu.make_async_copy(nm_ref, nm_out.at[net.d], sems.at[4]),
-        ]
+        own = [pltpu.make_async_copy(att_ref, att_out.at[net.x, net.y, net.d], sems.at[0])]
         att_plane.start()
         shared(net.x, net.y).start(att_ref)
-        gu_plane.start()
-        dn_plane.start()
         local(own)
         for k in range(1, gy):
             att_plane.relay(k)
@@ -309,37 +303,18 @@
                 att_plane.settle(j, k)
                 side, row = net.at_gx(j), net.at_gy(k)
                 shared(side, row).start(att_out.at[side, row, net.d])
-        for ref, item in tokens:
-            item.start(ref)
-        for k in range(1, gy):
-            gu_plane.relay(k)
-            dn_plane.relay(k)
         places = [(j, k) for j in range(gx) for k in range(gy)]
         for j, k in places:
             shared(net.at_gx(j), net.at_gy(k)).relay()
-        for _, item in tokens:
-            item.relay()
-        for j in range(1, gx):
-            for k in range(gy):
-                gu_plane.settle(j, k)
-                dn_plane.settle(j, k)
         for j, k in places:
             shared(net.at_gx(j), net.at_gy(k)).settle()
-        for _, item in tokens:
-            item.settle()
         wait_local(own)
 
-    shapes = (
-        jax.ShapeDtypeStruct((gx, gy, dp) + att.shape, BF16),
-        jax.ShapeDtypeStruct((gx, 2, gy) + gate_up.shape[1:], BF16),
-        jax.ShapeDtypeStruct((gx, gy) + down.shape, BF16),
-        jax.ShapeDtypeStruct((dp,) + cot.shape, BF16),
-        jax.ShapeDtypeStruct((dp,) + normed.shape, BF16),
-    )
+    shape = jax.ShapeDtypeStruct((gx, gy, dp) + att.shape, BF16)
     return call(
-        kernel, sizes, 1, "gather_weights", shapes, [ANY] * 5, [VMEM] * 5,
-        [pltpu.SemaphoreType.DMA((5,))], sends, slots,
-    )(att, gate_up, down, cot, normed)
+        kernel, sizes, 1, "gather_weights", shape, ANY, [VMEM], [pltpu.SemaphoreType.DMA((1,))],
+        gx * gy * (hops + dp) + gx * gy + gy, gx * gy * (hops + dp) + gy + gx * gy,
+    )(att)
 
 
 def turned(values):
@@ -363,10 +338,10 @@
         ref[:, lanes] = values[n * rows : (n + 1) * rows].astype(ref.dtype)
 
 
-def attend_heads(q_ref, kv_ref, bias_ref, mixed_ref, logsum_ref):
+def attend_heads(key_heads, q_ref, kv_ref, bias_ref, mixed_ref, logsum_ref):
     rows = q_ref.shape[0]
     bias = jnp.concatenate([bias_ref[...]] * GROUPS, axis=1)
-    for k in range(KEY_VALUE_HEADS):
+    for k in key_heads:
         query = head_rows(q_ref, k * GROUPS)
         scores = back_product(key_columns(kv_ref, k), query) * HEAD_WIDTH ** (-0.5) + bias
         highest = jnp.max(scores, axis=0, keepdims=True)
@@ -403,33 +378,137 @@
         dkv_ref[:, :, :, lanes] = dvalues.astype(BF16).reshape(blocks + (HEAD_WIDTH,))
 
 
-def attend(sizes, query, piece, bias):
+def turn_pairs(values, cos, sin):
+    lanes = cos.shape[1]
+    half = HEAD_WIDTH // 2
+    front = lax.broadcasted_iota(jnp.int32, cos.shape, 1) % HEAD_WIDTH < half
+    pieces = []
+    for first in range(0, values.shape[1], lanes):
+        part = values[:, first : first + lanes]
+        other = jnp.where(front, pltpu.roll(part, lanes - half, 1), pltpu.roll(part, half, 1))
+        pieces.append(part * cos + other * sin)
+    return jnp.concatenate(pieces, axis=1)
+
+
+def forward(sizes, cols, att, normed, inputs, gain, cos, sin, bias, gate_up, down, cot):
     dp, gx, gy = sizes
-
-    def kernel(net, q_ref, src, bias_ref, out, mixed_ref, logsum_ref, sems):
-        net.greet(net.plane_peers())
-        plane = PlaneGather(net, src, lambda a, b: out.at[a, b])
-        own = [pltpu.make_async_copy(src, out.at[net.x, net.y], sems.at[0])]
-        plane.start()
+    q_cols, k_cols, v_cols, o_cols = cols
+    qkv_cols = q_cols + k_cols + v_cols
+    rows, width = inputs.shape
+    fan = att.shape[3]
+    lanes = cos.shape[1]
+    q_width, k_width, v_width = gy * q_cols, gy * k_cols, gy * v_cols
+    q_pad, k_pad = -(-q_width // lanes) * lanes, -(-k_width // lanes) * lanes
+
+    def kernel(
+        net, att_ref, nm_ref, in_ref, gain_ref, cos_ref, sin_ref, bias_ref, gu_ref, dn_ref, cot_ref,
+        q_ref, kv_out, mixed_ref, logsum_ref, hidden_ref,
+        gu_out, dn_out, cot_out, nm_out, mixed_out, two_out,
+        q_wide, k_wide, kv_ref, two_ref, sems,
+    ):
+        q_wide[...] = jnp.zeros_like(q_wide)
+        k_wide[...] = jnp.zeros_like(k_wide)
+        for b in range(gy):
+            block = sum(
+                back_product(nm_ref[:, a * fan : (a + 1) * fan], att_ref[a, b, :qkv_cols, :])
+                for a in range(gx)
+            ).astype(BF16)
+            q_wide[:, b * q_cols : (b + 1) * q_cols] = block[:, :q_cols].astype(F32)
+            k_wide[:, b * k_cols : (b + 1) * k_cols] = block[:, q_cols : q_cols + k_cols].astype(F32)
+            first = k_width + b * v_cols
+            kv_ref[:, first : first + v_cols] = block[:, q_cols + k_cols :]
+        cos_rows, sin_rows = cos_ref[...], sin_ref[...]
+        kv_ref[:, :k_width] = turn_pairs(k_wide[...], cos_rows, sin_rows)[:, :k_width].astype(BF16)
+
+        net.greet(net.plane_peers() + net.share_peers())
+        kv = PlaneGather(net, kv_ref, lambda a, b: kv_out.at[a, b])
+        gu = PlaneGather(net, gu_ref, lambda a, b: gu_out.at[a, :, b])
+        dn = PlaneGather(net, dn_ref, lambda a, b: dn_out.at[a, b])
+        cot_share, nm_share, mixed_share, two_share = (
+            Share(net, lambda r, out=out: out.at[r]) for out in (cot_out, nm_out, mixed_out, two_out)
+        )
+        own = [
+            pltpu.make_async_copy(kv_ref, kv_out.at[net.x, net.y], sems.at[0]),
+            pltpu.make_async_copy(gu_ref, gu_out.at[net.x, :, net.y], sems.at[1]),
+            pltpu.make_async_copy(dn_ref, dn_out.at[net.x, net.y], sems.at[2]),
+            pltpu.make_async_copy(cot_ref, cot_out.at[net.d], sems.at[3]),
+            pltpu.make_async_copy(nm_ref, nm_out.at[net.d], sems.at[4]),
+        ]
+        kv.start()
+        gu.start_gy()
+        dn.start_gy()
         local(own)
+        cot_share.start(cot_ref)
+        nm_share.start(nm_ref)
+        q_ref[...] = turn_pairs(q_wide[...], cos_rows, sin_rows)[:, :q_width].astype(BF16)
         for k in range(1, gy):
-            plane.relay(k)
+            kv.relay(k)
+        gu.start_gx()
+        dn.start_gx()
         for j in range(1, gx):
             for k in range(gy):
-                plane.settle(j, k)
+                kv.settle(j, k)
         wait_local(own)
-        attend_heads(q_ref, out, bias_ref, mixed_ref, logsum_ref)
-
-    rows = query.shape[0]
+
+        turns = list(range(1, gy))
+        heads = list(range(KEY_VALUE_HEADS))
+        for n, k in enumerate(turns):
+            mine = heads[n * len(heads) // len(turns) : (n + 1) * len(heads) // len(turns)]
+            attend_heads(mine, q_ref, kv_out, bias_ref, mixed_ref, logsum_ref)
+            if n + 1 < len(turns):
+                gu.relay(k)
+                dn.relay(k)
+        last = pltpu.make_async_copy(mixed_ref, mixed_out.at[net.d], sems.at[5])
+        last.start()
+        mixed_share.start(mixed_ref)
+        for b in range(gy):
+            block = sum(
+                back_product(mixed_ref[:, a * fan : (a + 1) * fan], att_ref[a, b, qkv_cols:, :])
+                for a in range(gx)
+            ).astype(BF16)
+            span = slice(b * o_cols, (b + 1) * o_cols)
+            hidden_ref[:, span] = in_ref[:, span].astype(F32) + block.astype(F32)
+        hidden = hidden_ref[...]
+        scale = lax.rsqrt(jnp.sum(hidden * hidden, axis=1, keepdims=True) / width + EPSILON)
+        two_ref[...] = (hidden * scale * gain_ref[...]).astype(BF16)
+        local_two = pltpu.make_async_copy(two_ref, two_out.at[net.d], sems.at[6])
+        local_two.start()
+        two_share.start(two_ref)
+        gu.relay(turns[-1])
+        dn.relay(turns[-1])
+        shares = (cot_share, nm_share, mixed_share, two_share)
+        for share in shares:
+            share.relay()
+        for share in shares:
+            share.settle()
+        for j in range(1, gx):
+            for k in range(gy):
+                gu.settle(j, k)
+                dn.settle(j, k)
+        wait_local([last, local_two])
+
+    shared = jax.ShapeDtypeStruct((dp,) + inputs.shape, BF16)
     shapes = (
-        jax.ShapeDtypeStruct((gx, gy) + piece.shape, piece.dtype),
-        jax.ShapeDtypeStruct(query.shape, BF16),
+        jax.ShapeDtypeStruct((rows, q_width), BF16),
+        jax.ShapeDtypeStruct((gx, gy, rows, k_width + v_width), BF16),
+        jax.ShapeDtypeStruct((rows, q_width), BF16),
         jax.ShapeDtypeStruct((KEY_VALUE_HEADS, GROUPS * rows), F32),
-    )
+        jax.ShapeDtypeStruct(inputs.shape, F32),
+        jax.ShapeDtypeStruct((gx, 2, gy) + gate_up.shape[1:], BF16),
+        jax.ShapeDtypeStruct((gx, gy) + down.shape, BF16),
+        shared, shared, shared, shared,
+    )
+    scratch = [
+        pltpu.VMEM((rows, q_pad), F32),
+        pltpu.VMEM((rows, k_pad), F32),
+        pltpu.VMEM((rows, k_width + v_width), BF16),
+        pltpu.VMEM(inputs.shape, BF16),
+        pltpu.SemaphoreType.DMA((7,)),
+    ]
+    count = 3 * (gx * gy + gy) + 4 * 2 * dp
     return call(
-        kernel, sizes, 2, "attend", shapes, [VMEM] * 3, [VMEM] * 3,
-        [pltpu.SemaphoreType.DMA((1,))], gx * gy + gy, gy + gx * gy,
-    )(query, piece, bias)
+        kernel, sizes, 2, "forward", shapes, [VMEM] * 5 + [ANY] * 6, [VMEM] * 10, scratch, count, count,
+    )(att, normed, inputs, gain, cos, sin, bias, gate_up, down, cot)
 
 
 def attend_back(query, kv_all, bias, logsum, mixed, dmixed):
@@ -494,34 +573,6 @@
         out_specs=[VMEM] * 4,
         scratch_shapes=[pltpu.VMEM((gx, rows, part), BF16), pltpu.VMEM((rows, both), BF16)],
     )(normed_all, cot_all, gate_up, down)
-
-
-def share_tokens(sizes, *pieces):
-    dp, gx, gy = sizes
-    count = len(pieces)
-
-    def kernel(net, *refs):
-        srcs, outs, sems = refs[:count], refs[count : 2 * count], refs[2 * count]
-        net.greet(net.share_peers())
-        items = [Share(net, lambda r, out=out: out.at[r]) for out in outs]
-        own = [
-            pltpu.make_async_copy(src, out.at[net.d], sems.at[n])
-            for n, (src, out) in enumerate(zip(srcs, outs))
-        ]
-        for item, src in zip(items, srcs):
-            item.start(src)
-        local(own)
-        for item in items:
-            item.relay()
-        for item in items:
-            item.settle()
-        wait_local(own)
-
-    shapes = tuple(jax.ShapeDtypeStruct((dp,) + p.shape, p.dtype) for p in pieces)
-    return call(
-        kernel, sizes, 3, "share_tokens", shapes, [ANY] * count, [VMEM] * count,
-        [pltpu.SemaphoreType.DMA((count,))], count * dp, count * (dp // 2 + dp),
-    )(*pieces)
 
 
 def sum_tokens(sizes, *parts):
@@ -761,45 +812,34 @@
         down_weight.reshape(groups, dp, share, down_cols), rank, 1, 1
     ).reshape(groups * share, down_cols).T
 
-    att_all, gate_up_all, down_all, cot_all, normed_one_all = gather_weights(
-        sizes, att_part, gate_up_part, down_part, cotangent, normed_one
-    )
-    att_all = att_all.reshape(gx, gy, all_cols, fan)
+    att_all = gather_weights(sizes, att_part).reshape(gx, gy, all_cols, fan)
+    cos_wide = jnp.tile(cos_table[:, 0], (1, 4))
+    sin_wide = jnp.tile(jnp.concatenate([-sin_table[:, 0], sin_table[:, 0]], axis=1), (1, 2))
+    (
+        rotated_query, kv_all, attention_mixture, logsum, hidden,
+        gate_up_all, down_all, cot_all, normed_one_all, mixed_all, normed_all,
+    ) = forward(
+        sizes, (q_cols, k_cols, v_cols, o_cols), att_all, normed_one, inputs, mlp_gain.reshape(1, -1),
+        cos_wide, sin_wide, bias, gate_up_part, down_part, cotangent,
+    )
+    kv_width = gy * k_cols
     qkv_rows = att_all[:, :, :qkv_cols].reshape(gx, gy * qkv_cols, fan)
     out_rows = att_all[:, :, qkv_cols:].reshape(gx, gy * o_cols, fan)
     hidden_width = gy * share
     gate_up_all = gate_up_all.reshape(gx, 2 * hidden_width, fan)
     half_hidden = groups * share
     down_all = down_all.reshape(gx, gy * down_cols, half_hidden)
-    cot_all = cot_all.reshape(dp * count_of_rows, width)
-    normed_one_all = normed_one_all.reshape(dp * count_of_rows, width)
+    cot_all, normed_one_all, mixed_all, normed_all = (
+        rows.reshape(dp * count_of_rows, width) for rows in (cot_all, normed_one_all, mixed_all, normed_all)
+    )
+    rms_two, unit_two, _ = normalize(hidden, mlp_gain)
 
     def parts(rows):
         return [rows[:, a * fan : (a + 1) * fan] for a in range(gx)]
 
-    def onto(rows, weights):
-        return sum(back_product(part, weights[a]) for a, part in enumerate(parts(rows)))
-
     def back_onto(rows, weights):
         return jnp.concatenate([plain_product(rows, weights[a]) for a in range(gx)], axis=1)
 
-    qkv = onto(normed_one, qkv_rows).astype(BF16).reshape(count_of_rows, gy, qkv_cols)
-    query_rows = qkv[:, :, :q_cols].reshape(count_of_rows, -1)
-    key_rows = qkv[:, :, q_cols : q_cols + k_cols].reshape(count_of_rows, -1)
-    value_rows = qkv[:, :, q_cols + k_cols :].reshape(count_of_rows, -1)
-    rotated_query = rotate(query_rows.astype(F32), cos_table, sin_table).astype(BF16)
-    rotated_key = rotate(key_rows.astype(F32), cos_table, sin_table).astype(BF16)
-    kv_width = rotated_key.shape[1]
-    kv_all, attention_mixture, logsum = attend(
-        sizes, rotated_query, jnp.concatenate([rotated_key, value_rows], axis=1), bias
-    )
-    attn_out = lax.optimization_barrier(onto(attention_mixture, out_rows).astype(BF16))
-    hidden = residual + attn_out.astype(F32)
-    rms_two, unit_two, normed_two = normalize(hidden, mlp_gain)
-
-    normed_all, mixed_all = share_tokens(sizes, normed_two, attention_mixture)
-    normed_all = normed_all.reshape(dp * count_of_rows, width)
-    mixed_all = mixed_all.reshape(dp * count_of_rows, width)
     dnormed_part, mlp_part, gate_up_grad, down_grad = mlp(normed_all, cot_all, gate_up_all, down_all)
     dnormed_two, mlp_out = sum_tokens(
         sizes,

time: 397 us -> 358 us (0.902)
  local copies, waits for them, and re-layouts: 48.9 us -> 30.6 us
  other arithmetic: 29.3 us -> 12.8 us
  matrix products: 12.6 us -> 8.57 us
    pallas_call x1, Pallas kernels: 21.5 us -> 30.8 us  [sum_plane(): call(kernel, sizes, 5, 'sum_plane', jax.ShapeDtypeStruct(shape, F32), VME...]
    pallas_call x3 -> x2, Pallas kernels: 138 us -> 131 us  [the longest x1 87 us: forward(): call(kernel, sizes, 2, 'forward', shapes, [VMEM] * 5 + [ANY] * 6, [VMEM]...]
    unnamed x92 -> x62, local copies, waits for them, and re-layouts: 14 us -> 9.18 us
where the time goes in v1:
time: 358 us; the launch traced here: 353 us
  Pallas kernels  300 us (84%)
  local copies, waits for them, and re-layouts  30.6 us (9%)
  other arithmetic  12.8 us (4%)
  matrix products  8.57 us (2%)
    pallas_call x1, Pallas kernels, forward(): call(kernel, sizes, 2, 'forward', shapes, [VMEM] * 5 + [ANY] * 6, [VMEM]...  87 us
    pallas_call x1, Pallas kernels, reduce_weights(): call(kernel, sizes, 7, 'reduce_weights', shapes, [ANY] * 4, [VMEM] * 4, s...  85.5 us
    pallas_call x1, Pallas kernels, gather_weights(): call(kernel, sizes, 1, 'gather_weights', shape, ANY, [VMEM], [pltpu.Semap...  44.3 us
    pallas_call x1, Pallas kernels, sum_plane(): call(kernel, sizes, 5, 'sum_plane', jax.ShapeDtypeStruct(shape, F32), VME...  30.8 us
    pallas_call x1, Pallas kernels, sum_tokens(): call(kernel, sizes, 4, 'sum_tokens', shapes, [VMEM] * count, [VMEM] * cou...  17.7 us
    pallas_call x1, Pallas kernels, trade_tokens(): call(kernel, sizes, 6, 'trade_tokens', jax.ShapeDtypeStruct(blocks.shape,...  13.6 us
    pallas_call x1, Pallas kernels, mlp(): pl.pallas_call(kernel, name='mlp', out_shape=(jax.ShapeDtypeStruct(normed...  12.8 us
    unnamed x62, local copies, waits for them, and re-layouts  9.18 us

profile of v1, /device:TPU:31, one launch (start us, length us, event | category | flops | bytes accessed | tf_op | source)
XLA Modules:
  0.0 353.4 jit_solution(16808653356673263035)
XLA Ops:
  1.4 1.7 fusion.21.refs_6_.bias_ref
  4.8 1.3 constant_dynamic-slice_fusion.1
  8.6 44.3 %gather_weights.1 = bf16[2,4,4,160,480]{4,3,2,1,0:T(8,128)(2,1)} custom-call(bf16[160,480]{1,0:T(8,128)(2,1)} %fusion.25.refs_0_), custom_call_target="tpu_custom_call" | custom-call | tf_op jit(solution)/shard_map/gather_weights/pallas_call | solution.py:314
  56.0 87.0 %forward.1 = (bf16[128,960]{1,0:T(8,128)(2,1)}, bf16[2,4,128,640]{3,2,1,0:T(8,128)(2,1)}, bf16[128,960]{1,0:T(8,128)(2,1)}, f32[5,384]{1,0:T(8,128)}, f32[128,96...) custom-call(bf16[2,4,640,480]{3,2,1,0:T(8,128)(2,1)} %bitcast.76, ...), custom_call_target="tpu_custom_call" | custom-call | tf_op jit(solution)/shard_map/forward/pallas_call | solution.py:509
  143.0 12.8 %mlp.1 = (bf16[512,960]{1,0:T(8,128)(2,1)}, bf16[512,960]{1,0:T(8,128)(2,1)}, bf16[2,1280,480]{2,1,0:T(8,128)(2,1)}, bf16[2,960,320]{2,1,0:T(8,128)(2,1)}) custom-call(bf16[512,960]{1,0:T(8,128)(2,1)} %bitcast.105, bf16[512,960]{1,0:T(8,128)(2,1)} %bitcast.104, bf16[2,1280,480]{2,1,0:T(8,128)(2,1)} %bitcast.92, bf16[2,960,320]{2,1,0:T(8,128)(2,1)} %bitcast.99), custom_call_target="tpu_custom_call" | custom-call | tf_op jit(solution)/shard_map/mlp/pallas_call | solution.py:563
  155.7 17.7 %sum_tokens.1 = (f32[128,960]{1,0:T(8,128)}, f32[128,960]{1,0:T(8,128)}) custom-call(bf16[4,128,960]{2,1,0:T(8,128)(2,1)} %bitcast.102, bf16[4,128,960]{2,1,0:T(8,128)(2,1)} %bitcast.103), custom_call_target="tpu_custom_call" | custom-call | tf_op jit(solution)/shard_map/sum_tokens/pallas_call | solution.py:619
  173.6 1.4 multiply_reduce_fusion
  175.2 1.7 fusion.31
  179.0 8.5 %attend_back.1 = (f32[128,960]{1,0:T(8,128)}, bf16[2,4,128,640]{3,2,1,0:T(8,128)(2,1)}) custom-call(bf16[128,960]{1,0:T(8,128)(2,1)} %get-tuple-element.43.q_ref, bf16[2,4,128,640]{3,2,1,0:T(8,128)(2,1)} %get-tuple-element.44.kv_ref, f32[1024,128]{1,0:T(8,128)} %fusion.21.refs_6_.bias_ref, f32[5,384]{1,0:T(8,128)} %get-tuple-element.45.logsum_ref, ...), custom_call_target="tpu_custom_call" | custom-call | tf_op jit(solution)/shard_map/attend_back/pallas_call | solution.py:515
  188.9 30.8 %sum_plane.1 = f32[128,640]{1,0:T(8,128)} custom-call(bf16[2,4,128,640]{3,2,1,0:T(8,128)(2,1)} %get-tuple-element.48.refs_0_), custom_call_target="tpu_custom_call" | custom-call | tf_op jit(solution)/shard_map/sum_plane/pallas_call | solution.py:640
  221.9 2.1 fusion.30
  228.4 13.6 %trade_tokens.1 = bf16[4,128,640]{2,1,0:T(8,128)(2,1)} custom-call(bf16[4,128,640]{2,1,0:T(8,128)(2,1)} %copy.101.refs_0_), custom_call_target="tpu_custom_call" | custom-call | tf_op jit(solution)/shard_map/trade_tokens/pallas_call | solution.py:663
  242.0 1.7 fusion.18
  243.8 1.6 fusion
  245.8 2.1 fusion.15
  249.1 1.3 pad_maximum_fusion.refs_2_
  250.4 85.5 %reduce_weights.1 = (bf16[4,2,160,480]{3,2,1,0:T(8,128)(2,1)}, bf16[4,240,320]{2,1,0:T(8,128)(2,1)}, bf16[4,160,480]{2,1,0:T(8,128)(2,1)}, f32[4,16,128]{2,1,0:T(8,128)}) custom-call(bf16[2,2,4,160,480]{4,3,2,1,0:T(8,128)(2,1)} %bitcast.91, bf16[2,4,240,320]{3,2,1,0:T(8,128)(2,1)} %bitcast.98, bf16[2,4,160,480]{3,2,1,0:T(8,128)(2,1)} %pad_maximum_fusion.refs_2_, ...), custom_call_target="tpu_custom_call" | custom-call | tf_op jit(solution)/shard_map/reduce_weights/pallas_call | solution.py:719
  335.9 1.4 fusion.32
  337.5 1.4 copy.105
  339.1 1.4 copy.106
  340.9 1.4 copy.113
  346.1 1.7 copy.111
  347.8 1.7 copy.112
  350.3 1.4 fusion.11
  (119 shorter events, 26.5 us)
Async XLA Ops:
  4.0 3.1 copy-start.14
  4.8 2.5 copy-start.15
  6.1 1.3 copy-start.18
  6.1 1.3 copy-start.19
  8.6 44.3 %copy-start.13 = (bf16[1280,240]{0,1:T(8,128)(2,1)S(1)}, bf16[1280,240]{0,1:T(8,128)(2,1)}, u32[]{:S(2)}) copy-start(bf16[1280,240]{0,1:T(8,128)(2,1)} %param.22) | copy-start | bytes 1843204
  52.8 1.1 copy-start.16
  52.9 1.4 copy-start.21
  52.9 2.2 copy-start.17
  54.1 1.9 copy-start
  155.7 17.8 %copy-start.2 = (f32[128,960]{1,0:T(8,128)S(1)}, f32[128,960]{1,0:T(8,128)}, u32[]{:S(2)}) copy-start(f32[128,960]{1,0:T(8,128)} %get-tuple-element.34) | copy-start | bytes 1474564
  155.7 17.9 %copy-start.20 = (f32[960]{0:T(1024)S(1)}, f32[960]{0:T(1024)}, u32[]{:S(2)}) copy-start(f32[960]{0:T(1024)} %param.19) | copy-start | bytes 11524
  173.5 1.5 copy-start.3
  173.5 1.5 copy-start.5
  224.5 1.3 copy-start.7
  224.5 1.0 copy-start.1
  227.3 14.7 %copy-start.24 = (bf16[4,128,960]{2,1,0:T(8,128)(2,1)S(1)}, bf16[4,128,960]{2,1,0:T(8,128)(2,1)}, u32[]{:S(2)}) copy-start(bf16[4,128,960]{2,1,0:T(8,128)(2,1)} %get-tuple-element.51) | copy-start | bytes 2949124
  242.0 1.9 copy-start.12
  245.8 2.1 copy-start.23
  339.1 1.4 copy-start.11
  345.1 4.5 %copy-start.22 = (f32[4,16,128]{2,1,0:T(8,128)S(1)}, f32[4,16,128]{2,1,0:T(8,128)}, u32[]{:S(2)}) copy-start(f32[4,16,128]{2,1,0:T(8,128)} %get-tuple-element.56) | copy-start | bytes 98308
  345.1 5.1 %copy-start.4 = (f32[128,960]{1,0:T(8,128)S(1)}, f32[128,960]{1,0:T(8,128)}, u32[]{:S(2)}) copy-start(f32[128,960]{1,0:T(8,128)} %get-tuple-element.42) | copy-start | bytes 1474564
  345.1 5.1 %copy-start.6 = (bf16[128,960]{1,0:T(8,128)(2,1)S(1)}, bf16[128,960]{1,0:T(8,128)(2,1)}, u32[]{:S(2)}) copy-start(bf16[128,960]{1,0:T(8,128)(2,1)} %copy.90.refs_9_) | copy-start | bytes 737284
  345.1 5.1 %copy-start.8 = (f32[128,480]{1,0:T(8,128)S(1)}, f32[128,480]{1,0:T(8,128)}, u32[]{:S(2)}) copy-start(f32[128,480]{1,0:T(8,128)} %copy-done.7) | copy-start | bytes 737284
  345.1 5.1 %copy-start.10 = (f32[128,480]{1,0:T(8,128)S(1)}, f32[128,480]{1,0:T(8,128)}, u32[]{:S(2)}) copy-start(f32[128,480]{1,0:T(8,128)} %copy-done.9) | copy-start | bytes 737284
  (1 other events, 0.7 us)

commit v2 on v1

--- a/solution.py
+++ b/solution.py
@@ -511,19 +511,6 @@
     )(att, normed, inputs, gain, cos, sin, bias, gate_up, down, cot)
 
 
-def attend_back(query, kv_all, bias, logsum, mixed, dmixed):
-    return pl.pallas_call(
-        attend_heads_back,
-        name="attend_back",
-        out_shape=(
-            jax.ShapeDtypeStruct(query.shape, F32),
-            jax.ShapeDtypeStruct(kv_all.shape, BF16),
-        ),
-        in_specs=[VMEM] * 6,
-        out_specs=[VMEM] * 2,
-    )(query, kv_all, bias, logsum, mixed, dmixed)
-
-
 def mlp(normed_all, cot_all, gate_up, down):
     gx, both, fan = gate_up.shape
     rows, width = normed_all.shape
@@ -622,83 +609,145 @@
     )(*parts)
 
 
-def sum_plane(sizes, blocks):
+def backward(
+    sizes, cols, query, kv_all, bias, logsum, mixed, dmixed, dhidden, att, normed_all, mixed_all,
+    inputs, gain, mlpgain, cos, sin, gate_up, down,
+):
     dp, gx, gy = sizes
-    shape = blocks.shape[2:]
-
-    def kernel(net, src, out, landing_x, stage, landing_y):
-        net.greet(net.plane_peers())
-        item = PlaneSum(net, lambda a, b: src.at[a, b], landing_x, stage, landing_y)
+    q_cols, k_cols, v_cols, o_cols = cols
+    qkv_cols = q_cols + k_cols + v_cols
+    all_cols = qkv_cols + o_cols
+    att_share = all_cols // dp
+    rows, width = inputs.shape
+    fan = att.shape[3]
+    lanes = cos.shape[1]
+    q_width, k_width = gy * q_cols, gy * k_cols
+    q_pad, k_pad = -(-q_width // lanes) * lanes, -(-k_width // lanes) * lanes
+    kv_width = kv_all.shape[3]
+    pieces = [
+        (gate_up.shape[3:], BF16), (gate_up.shape[3:], BF16), (down.shape[2:], BF16),
+        ((att_share, fan), BF16), ((8, width), F32), ((rows, kv_width), BF16),
+    ]
+    count = len(pieces)
+
+    def kernel(net, *refs):
+        (
+            q_ref, kv_ref, bias_ref, logsum_ref, mixed_ref, dmixed_ref, dhidden_ref, att_ref, nm_ref,
+            mx_ref, in_ref, gain_ref, mlpgain_ref, cos_ref, sin_ref, gu_ref, dn_ref,
+        ) = refs[:17]
+        input_grad, gu_out, dn_out, att_out, gain_out = refs[17:22]
+        q_wide, k_wide, dkv_ref, p_ref, trade_src, trade_in, dn_one, att_grad, gains = refs[22:31]
+        refs = refs[31:]
+        landing_x, stage, landing_y = (refs[n * count : (n + 1) * count] for n in range(3))
+        result, sems = refs[3 * count : 4 * count - 1], refs[4 * count - 1]
+
+        net.greet(net.plane_peers() + [net.dp_peer(i) for i in range(1, dp)])
+        sources = [
+            lambda a, b: gu_ref.at[a, 0, b], lambda a, b: gu_ref.at[a, 1, b], lambda a, b: dn_ref.at[a, b],
+            lambda a, b: att_grad.at[a, b], lambda a, b: gains, lambda a, b: dkv_ref.at[a, b],
+        ]
+        sums = [
+            PlaneSum(net, sources[n], landing_x[n], stage[n], landing_y[n]) for n in range(count)
+        ]
+        outs = [
+            lambda r: gu_out.at[r, 0], lambda r: gu_out.at[r, 1], lambda r: dn_out.at[r],
+            lambda r: att_out.at[r], lambda r: gain_out.at[r],
+        ]
+        shares = [Share(net, out) for out in outs]
+        mlp_sums, att_sums, dkv_sum = sums[:3], sums[3:5], sums[5]
         order = far_first(gy) + [0]
-        for k in order:
-            item.start(k)
-        for k in order:
-            item.relay(k)
-        out[...] = item.total()
-
-    slab = pltpu.VMEM((gy,) + shape, BF16)
-    return call(
-        kernel, sizes, 5, "sum_plane", jax.ShapeDtypeStruct(shape, F32), VMEM, [VMEM],
-        [pltpu.VMEM((gx, gy) + shape, BF16), slab, slab], gx * gy + gy, gx * gy + gy,
-    )(blocks)
-
-
-def trade_tokens(sizes, blocks):
-    dp, gx, gy = sizes
-
-    def kernel(net, src, out, sems):
-        peers = [net.dp_peer(i) for i in range(1, dp)]
-        net.greet(peers)
-        slot = net.block(dp)
+
+        def begin(items, turns):
+            for k in turns:
+                for item in items:
+                    item.start(k)
+
+        def relay(items, turns):
+            for k in turns:
+                for item in items:
+                    item.relay(k)
+
+        own = []
+
+        def finish(first, items):
+            for n, item in enumerate(items, first):
+                result[n][...] = item.total().astype(result[n].dtype)
+                shares[n].start(result[n])
+                own.append(pltpu.make_async_copy(result[n], shares[n].out(net.d), sems.at[n]))
+                own[-1].start()
+
+        begin(mlp_sums, order[:1])
+        q_wide[...] = jnp.zeros_like(q_wide)
+        k_wide[...] = jnp.zeros_like(k_wide)
+        attend_heads_back(
+            q_ref, kv_ref, bias_ref, logsum_ref, mixed_ref, dmixed_ref, q_wide, dkv_ref
+        )
+        begin([dkv_sum], order)
+        begin(mlp_sums, order[1:2])
+        relay(mlp_sums, order[:1])
+        relay([dkv_sum], order)
+        begin(mlp_sums, order[2:])
+        cos_rows, sin_rows = cos_ref[...], -sin_ref[...]
+        dquery = turn_pairs(q_wide[...], cos_rows, sin_rows)[:, :q_width].astype(BF16)
+        dhidden = dhidden_ref[...]
+        dhidden_bf = dhidden.astype(BF16)
+        for b in range(gy):
+            p_ref[b, :, :q_cols] = dquery[:, b * q_cols : (b + 1) * q_cols]
+            p_ref[b, :, qkv_cols:] = dhidden_bf[:, b * o_cols : (b + 1) * o_cols]
+        dkv = dkv_sum.total()
+        k_wide[:, :k_width] = dkv[:, :k_width]
+        dkey = turn_pairs(k_wide[...], cos_rows, sin_rows)[:, :k_width].astype(BF16)
+        dvalue = dkv[:, k_width:].astype(BF16)
+        for b in range(gy):
+            p_ref[b, :, q_cols : q_cols + k_cols] = dkey[:, b * k_cols : (b + 1) * k_cols]
+            p_ref[b, :, q_cols + k_cols : qkv_cols] = dvalue[:, b * v_cols : (b + 1) * v_cols]
+        for r in range(dp):
+            for b in range(gy):
+                trade_src[r, :, b * att_share : (b + 1) * att_share] = p_ref[
+                    b, :, r * att_share : (r + 1) * att_share
+                ]
+        trade_slot = net.block(dp)
         for i in range(1, dp):
             rank = lax.rem(net.d + i, dp)
-            net.send(src.at[rank], out.at[net.d], slot + net.d, net.dp_peer(i))
-        own = pltpu.make_async_copy(src.at[net.d], out.at[net.d], sems.at[0])
-        own.start()
+            net.send(trade_src.at[rank], trade_in.at[net.d], trade_slot + net.d, net.dp_peer(i))
+        trade_in[net.d] = trade_src[net.d]
+        relay(mlp_sums, order[1:2])
+
+        for a in range(gx):
+            dn_one[:, a * fan : (a + 1) * fan] = sum(
+                plain_product(p_ref[b, :, :qkv_cols], att_ref[a, b, :qkv_cols, :]) for b in range(gy)
+            )
+        dnormed = dn_one[...]
+        values = in_ref[...].astype(F32)
+        rms = lax.rsqrt(jnp.sum(values * values, axis=1, keepdims=True) / width + EPSILON)
+        unit = values * rms
+        scaled = dnormed * gain_ref[...]
+        level = jnp.sum(scaled * unit, axis=1, keepdims=True) / width
+        input_grad[...] = (dhidden + rms * (scaled - unit * level)).astype(BF16)
+        gains[...] = jnp.zeros_like(gains)
+        gains[0:1, :] = jnp.sum(dnormed * unit, axis=0, keepdims=True)
+        gains[1:2, :] = mlpgain_ref[...]
+
         for i in range(1, dp):
             rank = lax.rem(net.d + i, dp)
-            net.arrive(out.at[rank], slot + rank)
-        own.wait()
-
-    return call(
-        kernel, sizes, 6, "trade_tokens", jax.ShapeDtypeStruct(blocks.shape, blocks.dtype), ANY, [VMEM],
-        [pltpu.SemaphoreType.DMA((1,))], dp, dp,
-    )(blocks)
-
-
-def reduce_weights(sizes, gate_up, down, att, gains):
-    dp, gx, gy = sizes
-    halves = gate_up.shape[1]
-    pieces = [gate_up.shape[3:]] * halves + [down.shape[2:], att.shape[2:]]
-    count = len(pieces)
-
-    def kernel(net, gu_ref, dn_ref, att_ref, gain_ref, *refs):
-        gu_out, dn_out, att_out, gain_out = refs[:4]
-        refs = refs[4:]
-        landing_x, stage, landing_y, result = (refs[n * (count + 1) : (n + 1) * (count + 1)] for n in range(4))
-        sems = refs[-1]
-        net.greet(net.plane_peers() + net.share_peers())
-        sources = [lambda a, b, n=n: gu_ref.at[a, n, b] for n in range(halves)]
-        sources += [lambda a, b: dn_ref.at[a, b], lambda a, b: att_ref.at[a, b], lambda a, b: gain_ref]
-        outs = [lambda r, n=n: gu_out.at[r, n] for n in range(halves)]
-        outs += [lambda r: dn_out.at[r], lambda r: att_out.at[r], lambda r: gain_out.at[r]]
-        sums = [
-            PlaneSum(net, sources[n], landing_x[n], stage[n], landing_y[n]) for n in range(count + 1)
-        ]
-        shares = [Share(net, out) for out in outs]
-        order = far_first(gy) + [0]
-        for k in order:
-            for item in sums:
-                item.start(k)
-        for k in order:
-            for item in sums:
-                item.relay(k)
-        own = []
-        for n, (item, share) in enumerate(zip(sums, shares)):
-            result[n][...] = item.total().astype(result[n].dtype)
-            share.start(result[n])
-            own.append(pltpu.make_async_copy(result[n], share.out(net.d), sems.at[n]))
-            own[-1].start()
+            net.arrive(trade_in.at[rank], trade_slot + rank)
+        dall = trade_in[...].reshape(dp * rows, gy * att_share)
+        places = lax.broadcasted_iota(jnp.int32, (gy * att_share, fan), 0) % att_share
+        from_normed = places + net.d * att_share < qkv_cols
+        for a in range(gx):
+            span = slice(a * fan, (a + 1) * fan)
+            grad = jnp.where(
+                from_normed,
+                weight_product(dall, nm_ref[:, span]),
+                weight_product(dall, mx_ref[:, span]),
+            ).astype(BF16)
+            for b in range(gy):
+                att_grad[a, b] = grad[b * att_share : (b + 1) * att_share]
+        begin(att_sums, order)
+        relay(mlp_sums, order[2:])
+        finish(0, mlp_sums)
+        relay(att_sums, order)
+        finish(3, att_sums)
         for share in shares:
             share.relay()
         for share in shares:
@@ -706,20 +755,34 @@
         wait_local(own)
 
     shapes = (
-        jax.ShapeDtypeStruct((dp, halves) + pieces[0], BF16),
-        jax.ShapeDtypeStruct((dp,) + pieces[-2], BF16),
-        jax.ShapeDtypeStruct((dp,) + pieces[-1], BF16),
-        jax.ShapeDtypeStruct((dp,) + gains.shape, F32),
-    )
-    kinds = [(piece, BF16) for piece in pieces] + [(gains.shape, F32)]
-    scratch = [pltpu.VMEM((gx, gy) + p, t) for p, t in kinds]
-    scratch += [pltpu.VMEM((gy,) + p, t) for p, t in kinds] * 2
-    scratch += [pltpu.VMEM(p, t) for p, t in kinds]
-    scratch += [pltpu.SemaphoreType.DMA((count + 1,))]
+        jax.ShapeDtypeStruct(inputs.shape, BF16),
+        jax.ShapeDtypeStruct((dp, 2) + pieces[0][0], BF16),
+        jax.ShapeDtypeStruct((dp,) + pieces[2][0], BF16),
+        jax.ShapeDtypeStruct((dp,) + pieces[3][0], BF16),
+        jax.ShapeDtypeStruct((dp,) + pieces[4][0], F32),
+    )
+    scratch = [
+        pltpu.VMEM((rows, q_pad), F32),
+        pltpu.VMEM((rows, k_pad), F32),
+        pltpu.VMEM(kv_all.shape, BF16),
+        pltpu.VMEM((gy, rows, all_cols), BF16),
+        pltpu.VMEM((dp, rows, gy * att_share), BF16),
+        pltpu.VMEM((dp, rows, gy * att_share), BF16),
+        pltpu.VMEM((rows, width), F32),
+        pltpu.VMEM((gx, gy, att_share, fan), BF16),
+        pltpu.VMEM((8, width), F32),
+    ]
+    scratch += [pltpu.VMEM((gx, gy) + p, t) for p, t in pieces]
+    scratch += [pltpu.VMEM((gy,) + p, t) for p, t in pieces] * 2
+    scratch += [pltpu.VMEM(p, t) for p, t in pieces[:-1]]
+    scratch += [pltpu.SemaphoreType.DMA((count - 1,))]
+    sems = count * (gx * gy + gy) + (count - 1) * 2 * dp + dp
     return call(
-        kernel, sizes, 7, "reduce_weights", shapes, [ANY] * 4, [VMEM] * 4, scratch,
-        (count + 1) * (gx * gy + gy + dp), (count + 1) * (gx * gy + gy + dp + dp // 2),
-    )(gate_up, down, att, gains)
+        kernel, sizes, 5, "backward", shapes, [VMEM] + [ANY] * 4, [VMEM] * 17, scratch, sems, sems,
+    )(
+        query, kv_all, bias, logsum, mixed, dmixed, dhidden, att, normed_all, mixed_all,
+        inputs, gain, mlpgain, cos, sin, gate_up, down,
+    )
 
 
 def rope_angles(positions):
@@ -727,26 +790,6 @@
     inverse = THETA ** (-(jnp.arange(half_dim, dtype=F32) * 2.0 / HEAD_WIDTH))
     angles = positions[:, None] * inverse[None, :]
     return (jnp.cos(angles)[:, None, :], jnp.sin(angles)[:, None, :])
-
-
-def rotate(values, cos_table, sin_table):
-    item_count = values.shape[0]
-    shaped = values.reshape(item_count, -1, HEAD_WIDTH)
-    half_dim = HEAD_WIDTH // 2
-    front_part = shaped[:, :, :half_dim]
-    back_part = shaped[:, :, half_dim:]
-    turned = jnp.concatenate(
-        [
-            front_part * cos_table - back_part * sin_table,
-            back_part * cos_table + front_part * sin_table,
-        ],
-        axis=2,
-    )
-    return turned.reshape(item_count, -1)
-
-
-def unrotate(values, cos_table, sin_table):
-    return rotate(values, cos_table, -sin_table)
 
 
 def normalize(values, gain):
@@ -789,7 +832,7 @@
     )
     bias = jnp.where(allowed, 0.0, MASKED).astype(F32)
     residual = inputs.astype(F32)
-    rms_one, unit_one, normed_one = normalize(residual, attn_gain)
+    _, _, normed_one = normalize(residual, attn_gain)
 
     fan = query_weight.shape[0]
     q_cols, k_cols, v_cols = query_weight.shape[1], key_weight.shape[1], value_weight.shape[1]
@@ -822,8 +865,6 @@
         sizes, (q_cols, k_cols, v_cols, o_cols), att_all, normed_one, inputs, mlp_gain.reshape(1, -1),
         cos_wide, sin_wide, bias, gate_up_part, down_part, cotangent,
     )
-    kv_width = gy * k_cols
-    qkv_rows = att_all[:, :, :qkv_cols].reshape(gx, gy * qkv_cols, fan)
     out_rows = att_all[:, :, qkv_cols:].reshape(gx, gy * o_cols, fan)
     hidden_width = gy * share
     gate_up_all = gate_up_all.reshape(gx, 2 * hidden_width, fan)
@@ -855,42 +896,10 @@
     dhidden = cotangent.astype(F32) + dhidden_norm
     dhidden_bf = dhidden.astype(BF16)
     mixture_gradient = back_onto(dhidden_bf, out_rows).astype(BF16)
-    dquery_rot, dkv = attend_back(
-        rotated_query, kv_all, bias, logsum, attention_mixture, mixture_gradient
-    )
-    dkv = sum_plane(sizes, dkv)
-    dquery = unrotate(dquery_rot, cos_table, sin_table).astype(BF16)
-    dkey = unrotate(dkv[:, :kv_width], cos_table, sin_table).astype(BF16)
-    dvalue_bf = dkv[:, kv_width:].astype(BF16)
-    dqkv = jnp.concatenate(
-        [
-            dquery.reshape(count_of_rows, gy, q_cols),
-            dkey.reshape(count_of_rows, gy, k_cols),
-            dvalue_bf.reshape(count_of_rows, gy, v_cols),
-        ],
-        axis=2,
-    )
-    dall = jnp.concatenate([dqkv, dhidden_bf.reshape(count_of_rows, gy, o_cols)], axis=2)
-    dall = dall.reshape(count_of_rows, gy, dp, att_share).transpose(2, 0, 1, 3)
-    dall = trade_tokens(sizes, dall.reshape(dp, count_of_rows, gy * att_share))
-    dall = dall.reshape(dp * count_of_rows, gy * att_share)
-    places = rank * att_share + lax.broadcasted_iota(jnp.int32, (gy, att_share, 1), 1)
-    from_normed = (places < qkv_cols).reshape(gy * att_share, 1)
-    att_grad = jnp.stack(
-        [
-            jnp.where(from_normed, weight_product(dall, one), weight_product(dall, two)).astype(BF16)
-            for one, two in zip(parts(normed_one_all), parts(mixed_all))
-        ]
-    ).reshape(gx, gy, att_share, fan)
-    dnormed_one = back_onto(dqkv.reshape(count_of_rows, gy * qkv_cols), qkv_rows)
-    dresidual, attgain_part = normalize_back(dnormed_one, attn_gain, rms_one, unit_one)
-    input_grad = (dhidden + dresidual).astype(BF16)
-    gain_parts = jnp.concatenate([attgain_part, mlpgain_part])
-    gain_rows = -(-gain_parts.shape[0] // 1024) * 8
-    gain_parts = jnp.pad(gain_parts, (0, gain_rows * 128 - gain_parts.shape[0])).reshape(gain_rows, 128)
-
-    gate_up_sum, down_sum, att_sum, gain_sum = reduce_weights(
-        sizes, gate_up_grad, down_grad, att_grad, gain_parts
+    input_grad, gate_up_sum, down_sum, att_sum, gain_sum = backward(
+        sizes, (q_cols, k_cols, v_cols, o_cols), rotated_query, kv_all, bias, logsum, attention_mixture,
+        mixture_gradient, dhidden, att_all, normed_one_all, mixed_all, inputs, attn_gain.reshape(1, -1),
+        mlpgain_part.reshape(1, -1), cos_wide, sin_wide, gate_up_grad, down_grad,
     )
     gate_grad = gate_up_sum[:, 0].reshape(dp * share, fan).T.astype(F32)
     up_grad = gate_up_sum[:, 1].reshape(dp * share, fan).T.astype(F32)
@@ -901,7 +910,7 @@
         .astype(F32)
     )
     att_sum = att_sum.reshape(all_cols, fan).T.astype(F32)
-    gains = jnp.sum(gain_sum, axis=0).reshape(-1)
+    gains = jnp.sum(gain_sum, axis=0)
     return (
         layer_out,
         input_grad,
@@ -912,8 +921,8 @@
         gate_grad,
         up_grad,
         down_grad,
-        gains[:width],
-        gains[width : 2 * width],
+        gains[0],
+        gains[1],
     )
 
 

time: 358 us -> 316 us (0.88); the launches traced: 353 us -> 315 us
  Pallas kernels: 300 us -> 285 us
  local copies, waits for them, and re-layouts: 30.6 us -> 19.9 us
  matrix products: 8.57 us -> 1.03 us
  other arithmetic: 12.8 us -> 8.5 us
    pallas_call x4 -> x1, Pallas kernels: 138 us -> 123 us  [backward(): call(kernel, sizes, 5, 'backward', shapes, [VMEM] + [ANY] * 4, [VMEM] * 1...]
    dot_general x4 -> x0, matrix products: 6.4 us -> none  [weight_product(): lax.dot_general(left, right, (((0,), (0,)), ((), ())), preferred_element_...]
    unnamed x62 -> x50, local copies, waits for them, and re-layouts: 9.18 us -> 6.53 us
where the time goes in v2:
time: 316 us; the launch traced here: 315 us
  Pallas kernels  285 us (90%)
  local copies, waits for them, and re-layouts  19.9 us (6%)
  other arithmetic  8.5 us (3%)
    pallas_call x1, Pallas kernels, backward(): call(kernel, sizes, 5, 'backward', shapes, [VMEM] + [ANY] * 4, [VMEM] * 1...  123 us
    pallas_call x1, Pallas kernels, forward(): call(kernel, sizes, 2, 'forward', shapes, [VMEM] * 5 + [ANY] * 6, [VMEM]...  86.9 us
    pallas_call x1, Pallas kernels, gather_weights(): call(kernel, sizes, 1, 'gather_weights', shape, ANY, [VMEM], [pltpu.Semap...  44.3 us
    pallas_call x1, Pallas kernels, sum_tokens(): call(kernel, sizes, 4, 'sum_tokens', shapes, [VMEM] * count, [VMEM] * cou...  17.7 us
    pallas_call x1, Pallas kernels, mlp(): pl.pallas_call(kernel, name='mlp', out_shape=(jax.ShapeDtypeStruct(normed...  12.8 us
    unnamed x50, local copies, waits for them, and re-layouts  6.53 us

profile of v2, /device:TPU:31, one launch (start us, length us, event | category | flops | bytes accessed | tf_op | source)
XLA Modules:
  0.0 315.3 jit_solution(2095315174149777267)
XLA Ops:
  0.7 0.8 dynamic_slice.16
  1.4 1.7 fusion.4.refs_6_.refs_2_
  4.8 1.3 constant_dynamic-slice_fusion.1
  7.4 1.1 fusion.8.refs_0_
  8.6 44.3 %gather_weights.1 = bf16[2,4,4,160,480]{4,3,2,1,0:T(8,128)(2,1)} custom-call(bf16[160,480]{1,0:T(8,128)(2,1)} %fusion.8.refs_0_), custom_call_target="tpu_custom_call" | custom-call | tf_op jit(solution)/shard_map/gather_weights/pallas_call | solution.py:314
  53.2 0.8 copy.76
  54.3 0.8 fusion.2.refs_1_
  55.1 0.9 copy.80.refs_9_
  56.0 86.9 %forward.1 = (bf16[128,960]{1,0:T(8,128)(2,1)}, bf16[2,4,128,640]{3,2,1,0:T(8,128)(2,1)}, bf16[128,960]{1,0:T(8,128)(2,1)}, f32[5,384]{1,0:T(8,128)}, f32[128,96...) custom-call(bf16[2,4,640,480]{3,2,1,0:T(8,128)(2,1)} %bitcast.49, ...), custom_call_target="tpu_custom_call" | custom-call | tf_op jit(solution)/shard_map/forward/pallas_call | solution.py:509
  142.9 12.8 %mlp.1 = (bf16[512,960]{1,0:T(8,128)(2,1)}, bf16[512,960]{1,0:T(8,128)(2,1)}, bf16[2,1280,480]{2,1,0:T(8,128)(2,1)}, bf16[2,960,320]{2,1,0:T(8,128)(2,1)}) custom-call(bf16[512,960]{1,0:T(8,128)(2,1)} %bitcast.69, bf16[512,960]{1,0:T(8,128)(2,1)} %bitcast.68, bf16[2,1280,480]{2,1,0:T(8,128)(2,1)} %bitcast.59, bf16[2,960,320]{2,1,0:T(8,128)(2,1)} %bitcast.61), custom_call_target="tpu_custom_call" | custom-call | tf_op jit(solution)/shard_map/mlp/pallas_call | solution.py:550
  155.7 17.7 %sum_tokens.1 = (f32[128,960]{1,0:T(8,128)}, f32[128,960]{1,0:T(8,128)}) custom-call(bf16[4,128,960]{2,1,0:T(8,128)(2,1)} %bitcast.66, bf16[4,128,960]{2,1,0:T(8,128)(2,1)} %bitcast.67), custom_call_target="tpu_custom_call" | custom-call | tf_op jit(solution)/shard_map/sum_tokens/pallas_call | solution.py:606
  173.6 2.0 multiply_reduce_fusion
  175.8 1.9 fusion.13
  179.0 0.8 pad_maximum_fusion.1.refs_5_
  179.8 123.2 %backward.1 = (bf16[128,960]{1,0:T(8,128)(2,1)}, bf16[4,2,160,480]{3,2,1,0:T(8,128)(2,1)}, bf16[4,240,320]{2,1,0:T(8,128)(2,1)}, bf16[4,160,480]{2,1,0:T(8,128)(2,1)}, f32[4,8,960]{2,1,0:T(8,128)}) custom-call(bf16[128,960]{1,0:T(8,128)(2,1)} %get-tuple-element.41.refs_0_, bf16[2,4,128,640]{3,2,1,0:T(8,128)(2,1)} %get-tuple-element.42.refs_1_, ...), custom_call_target="tpu_custom_call" | custom-call | tf_op jit(solution)/shard_map/backward/pallas_call | solution.py:780
  303.1 1.4 fusion.14
  304.7 1.4 copy.88
  306.3 1.4 copy.89
  308.1 1.4 copy.96
  310.2 1.1 fusion.15
  311.4 0.8 copy.94
  312.2 0.8 copy.95
  313.0 0.8 copy.93
  314.5 0.8 copy.92
  (73 shorter events, 7.3 us)
Async XLA Ops:
  4.0 3.1 copy-start.10
  4.8 2.5 copy-start.11
  6.1 1.3 copy-start.15
  6.1 1.3 copy-start.16
  8.6 44.3 %copy-start.7 = (bf16[1280,240]{0,1:T(8,128)(2,1)S(1)}, bf16[1280,240]{0,1:T(8,128)(2,1)}, u32[]{:S(2)}) copy-start(bf16[1280,240]{0,1:T(8,128)(2,1)} %param.22) | copy-start | bytes 1843204
  52.9 1.1 copy-start.12
  52.9 1.4 copy-start.18
  52.9 2.2 copy-start.13
  54.1 1.9 copy-start.1
  155.7 17.8 %copy-start.2 = (f32[128,960]{1,0:T(8,128)S(1)}, f32[128,960]{1,0:T(8,128)}, u32[]{:S(2)}) copy-start(f32[128,960]{1,0:T(8,128)} %get-tuple-element.33) | copy-start | bytes 1474564
  155.7 17.9 %copy-start.17 = (f32[960]{0:T(1024)S(1)}, f32[960]{0:T(1024)}, u32[]{:S(2)}) copy-start(f32[960]{0:T(1024)} %param.19) | copy-start | bytes 11524
  173.4 2.2 copy-start.3
  173.4 2.1 copy-start.4
  173.5 2.1 copy-start.8
  175.8 2.5 copy-start
  306.3 1.4 copy-start.5
  308.1 1.4 copy-start.6
  311.3 1.8 copy-start.9
  311.3 2.6 copy-start.14

commit v3 on v2

--- a/solution.py
+++ b/solution.py
@@ -242,6 +242,57 @@
         return total
 
 
+class TokenSum:
+    def __init__(self, net, src, mine, landing_core, landing_hop, sems):
+        self.net, self.src, self.mine, self.sems = net, src, mine, sems
+        self.landing_core, self.landing_hop = landing_core, landing_hop
+        self.core_slot = net.block(net.hops)
+        self.hop_slot = net.block(net.hops)
+        self.order = list(range(1, net.hops)) + [0]
+
+    def fetch(self, n):
+        net = self.net
+        rank = net.at_hop(self.order[n]) * net.cores + net.core
+        return pltpu.make_async_copy(self.src.at[rank], self.mine.at[n % 2], self.sems.at[n % 2])
+
+    def start(self):
+        net = self.net
+        for n in range(min(2, net.hops)):
+            self.fetch(n).start()
+        for i in self.order:
+            hop = net.at_hop(i)
+            net.send(
+                self.src.at[hop * net.cores + 1 - net.core], self.landing_core.at[hop],
+                self.core_slot + hop, net.core_peer(),
+            )
+
+    def relay(self):
+        net = self.net
+        for n, i in enumerate(self.order):
+            hop = net.at_hop(i)
+            self.fetch(n).wait()
+            net.arrive(self.landing_core.at[hop], self.core_slot + hop)
+            if i > 0:
+                total = self.mine[n % 2].astype(F32) + self.landing_core[hop].astype(F32)
+                self.landing_core[hop] = total.astype(BF16)
+                net.send(
+                    self.landing_core.at[hop], self.landing_hop.at[net.hop],
+                    self.hop_slot + net.hop, net.hop_peer(i),
+                )
+            if n + 2 < net.hops:
+                self.fetch(n + 2).start()
+
+    def total(self):
+        net = self.net
+        own = self.mine[(net.hops - 1) % 2].astype(F32)
+        total = own + self.landing_core[net.hop].astype(F32)
+        for i in range(1, net.hops):
+            hop = net.at_hop(i)
+            net.arrive(self.landing_hop.at[hop], self.hop_slot + hop)
+            total = total + self.landing_hop[hop].astype(F32)
+        return total
+
+
 def call(kernel, sizes, number, name, out_shapes, out_specs, in_specs, scratch, sends, slots):
     def body(*refs):
         net = Net(sizes, refs[-2], refs[-1])
@@ -271,13 +322,14 @@
         copy.wait()
 
 
-def gather_weights(sizes, att):
+def gather_weights(sizes, att, gate_up):
     dp, gx, gy = sizes
     hops = dp // 2
 
-    def kernel(net, att_ref, att_out, sems):
+    def kernel(net, att_ref, gu_ref, att_out, gu_out, sems):
         net.greet(net.plane_peers() + net.share_peers())
         att_plane = PlaneGather(net, att_ref, lambda a, b: att_out.at[a, b, net.d])
+        gu_plane = PlaneGather(net, gu_ref, lambda a, b: gu_out.at[a, :, b])
         first_hop = net.block(gx * gy * net.hops)
         first_core = net.block(gx * gy * net.dp)
 
@@ -290,31 +342,45 @@
             item.core_slot = first_core + place * net.dp
             return item
 
-        own = [pltpu.make_async_copy(att_ref, att_out.at[net.x, net.y, net.d], sems.at[0])]
+        own = [
+            pltpu.make_async_copy(att_ref, att_out.at[net.x, net.y, net.d], sems.at[0]),
+            pltpu.make_async_copy(gu_ref, gu_out.at[net.x, :, net.y], sems.at[1]),
+        ]
         att_plane.start()
         shared(net.x, net.y).start(att_ref)
+        gu_plane.start_gy()
         local(own)
         for k in range(1, gy):
             att_plane.relay(k)
             row = net.at_gy(k)
             shared(net.x, row).start(att_out.at[net.x, row, net.d])
+        gu_plane.start_gx()
         for j in range(1, gx):
             for k in range(gy):
                 att_plane.settle(j, k)
                 side, row = net.at_gx(j), net.at_gy(k)
                 shared(side, row).start(att_out.at[side, row, net.d])
         places = [(j, k) for j in range(gx) for k in range(gy)]
-        for j, k in places:
+        for n, (j, k) in enumerate(places):
             shared(net.at_gx(j), net.at_gy(k)).relay()
+            if n % 2 == 1 and n // 2 + 1 < gy:
+                gu_plane.relay(n // 2 + 1)
         for j, k in places:
             shared(net.at_gx(j), net.at_gy(k)).settle()
+        for j in range(1, gx):
+            for k in range(gy):
+                gu_plane.settle(j, k)
         wait_local(own)
 
-    shape = jax.ShapeDtypeStruct((gx, gy, dp) + att.shape, BF16)
+    shapes = (
+        jax.ShapeDtypeStruct((gx, gy, dp) + att.shape, BF16),
+        jax.ShapeDtypeStruct((gx, 2, gy) + gate_up.shape[1:], BF16),
+    )
+    count = gx * gy * (hops + dp) + 2 * (gx * gy + gy)
     return call(
-        kernel, sizes, 1, "gather_weights", shape, ANY, [VMEM], [pltpu.SemaphoreType.DMA((1,))],
-        gx * gy * (hops + dp) + gx * gy + gy, gx * gy * (hops + dp) + gy + gx * gy,
-    )(att)
+        kernel, sizes, 1, "gather_weights", shapes, [ANY] * 2, [VMEM] * 2,
+        [pltpu.SemaphoreType.DMA((2,))], count, count,
+    )(att, gate_up)
 
 
 def turned(values):
@@ -390,7 +456,7 @@
     return jnp.concatenate(pieces, axis=1)
 
 
-def forward(sizes, cols, att, normed, inputs, gain, cos, sin, bias, gate_up, down, cot):
+def forward(sizes, cols, att, normed, inputs, gain, cos, sin, bias, down, cot):
     dp, gx, gy = sizes
     q_cols, k_cols, v_cols, o_cols = cols
     qkv_cols = q_cols + k_cols + v_cols
@@ -401,9 +467,9 @@
     q_pad, k_pad = -(-q_width // lanes) * lanes, -(-k_width // lanes) * lanes
 
     def kernel(
-        net, att_ref, nm_ref, in_ref, gain_ref, cos_ref, sin_ref, bias_ref, gu_ref, dn_ref, cot_ref,
+        net, att_ref, nm_ref, in_ref, gain_ref, cos_ref, sin_ref, bias_ref, dn_ref, cot_ref,
         q_ref, kv_out, mixed_ref, logsum_ref, hidden_ref,
-        gu_out, dn_out, cot_out, nm_out, mixed_out, two_out,
+        dn_out, cot_out, nm_out, mixed_out, two_out,
         q_wide, k_wide, kv_ref, two_ref, sems,
     ):
         q_wide[...] = jnp.zeros_like(q_wide)
@@ -422,20 +488,17 @@
 
         net.greet(net.plane_peers() + net.share_peers())
         kv = PlaneGather(net, kv_ref, lambda a, b: kv_out.at[a, b])
-        gu = PlaneGather(net, gu_ref, lambda a, b: gu_out.at[a, :, b])
         dn = PlaneGather(net, dn_ref, lambda a, b: dn_out.at[a, b])
         cot_share, nm_share, mixed_share, two_share = (
             Share(net, lambda r, out=out: out.at[r]) for out in (cot_out, nm_out, mixed_out, two_out)
         )
         own = [
             pltpu.make_async_copy(kv_ref, kv_out.at[net.x, net.y], sems.at[0]),
-            pltpu.make_async_copy(gu_ref, gu_out.at[net.x, :, net.y], sems.at[1]),
             pltpu.make_async_copy(dn_ref, dn_out.at[net.x, net.y], sems.at[2]),
             pltpu.make_async_copy(cot_ref, cot_out.at[net.d], sems.at[3]),
             pltpu.make_async_copy(nm_ref, nm_out.at[net.d], sems.at[4]),
         ]
         kv.start()
-        gu.start_gy()
         dn.start_gy()
         local(own)
         cot_share.start(cot_ref)
@@ -443,7 +506,6 @@
         q_ref[...] = turn_pairs(q_wide[...], cos_rows, sin_rows)[:, :q_width].astype(BF16)
         for k in range(1, gy):
             kv.relay(k)
-        gu.start_gx()
         dn.start_gx()
         for j in range(1, gx):
             for k in range(gy):
@@ -456,7 +518,6 @@
             mine = heads[n * len(heads) // len(turns) : (n + 1) * len(heads) // len(turns)]
             attend_heads(mine, q_ref, kv_out, bias_ref, mixed_ref, logsum_ref)
             if n + 1 < len(turns):
-                gu.relay(k)
                 dn.relay(k)
         last = pltpu.make_async_copy(mixed_ref, mixed_out.at[net.d], sems.at[5])
         last.start()
@@ -474,7 +535,6 @@
         local_two = pltpu.make_async_copy(two_ref, two_out.at[net.d], sems.at[6])
         local_two.start()
         two_share.start(two_ref)
-        gu.relay(turns[-1])
         dn.relay(turns[-1])
         shares = (cot_share, nm_share, mixed_share, two_share)
         for share in shares:
@@ -483,7 +543,6 @@
             share.settle()
         for j in range(1, gx):
             for k in range(gy):
-                gu.settle(j, k)
                 dn.settle(j, k)
         wait_local([last, local_two])
 
@@ -494,7 +553,6 @@
         jax.ShapeDtypeStruct((rows, q_width), BF16),
         jax.ShapeDtypeStruct((KEY_VALUE_HEADS, GROUPS * rows), F32),
         jax.ShapeDtypeStruct(inputs.shape, F32),
-        jax.ShapeDtypeStruct((gx, 2, gy) + gate_up.shape[1:], BF16),
         jax.ShapeDtypeStruct((gx, gy) + down.shape, BF16),
         shared, shared, shared, shared,
     )
@@ -507,8 +565,8 @@
     ]
     count = 3 * (gx * gy + gy) + 4 * 2 * dp
     return call(
-        kernel, sizes, 2, "forward", shapes, [VMEM] * 5 + [ANY] * 6, [VMEM] * 10, scratch, count, count,
-    )(att, normed, inputs, gain, cos, sin, bias, gate_up, down, cot)
+        kernel, sizes, 2, "forward", shapes, [VMEM] * 5 + [ANY] * 5, [VMEM] * 9, scratch, count, count,
+    )(att, normed, inputs, gain, cos, sin, bias, down, cot)
 
 
 def mlp(normed_all, cot_all, gate_up, down):
@@ -562,56 +620,9 @@
     )(normed_all, cot_all, gate_up, down)
 
 
-def sum_tokens(sizes, *parts):
-    dp, gx, gy = sizes
-    count = len(parts)
-    hops = dp // 2
-    shape = parts[0].shape[1:]
-
-    def kernel(net, *refs):
-        srcs, outs, scratch = refs[:count], refs[count : 2 * count], refs[2 * count :]
-        landing_core, stage, landing_hop = scratch[:count], scratch[count : 2 * count], scratch[2 * count :]
-        net.greet(net.share_peers())
-        core_slots = [net.block(net.hops) for _ in range(count)]
-        hop_slots = [net.block(net.hops) for _ in range(count)]
-        order = list(range(1, net.hops)) + [0]
-        for n in range(count):
-            for i in order:
-                hop = net.at_hop(i)
-                net.send(
-                    srcs[n].at[hop * 2 + 1 - net.core], landing_core[n].at[hop],
-                    core_slots[n] + hop, net.core_peer(),
-                )
-        for n in range(count):
-            for i in order:
-                hop = net.at_hop(i)
-                net.arrive(landing_core[n].at[hop], core_slots[n] + hop)
-                total = srcs[n][hop * 2 + net.core].astype(F32) + landing_core[n][hop].astype(F32)
-                if i == 0:
-                    outs[n][...] = total
-                else:
-                    stage[n][hop] = total.astype(BF16)
-                    net.send(
-                        stage[n].at[hop], landing_hop[n].at[net.hop],
-                        hop_slots[n] + net.hop, net.hop_peer(i),
-                    )
-        for n in range(count):
-            for i in range(1, net.hops):
-                hop = net.at_hop(i)
-                net.arrive(landing_hop[n].at[hop], hop_slots[n] + hop)
-                outs[n][...] += landing_hop[n][hop].astype(F32)
-
-    shapes = tuple(jax.ShapeDtypeStruct(shape, F32) for _ in parts)
-    slab = pltpu.VMEM((hops,) + shape, BF16)
-    return call(
-        kernel, sizes, 4, "sum_tokens", shapes, [VMEM] * count, [VMEM] * count,
-        [slab] * (3 * count), count * dp, count * dp,
-    )(*parts)
-
-
 def backward(
-    sizes, cols, query, kv_all, bias, logsum, mixed, dmixed, dhidden, att, normed_all, mixed_all,
-    inputs, gain, mlpgain, cos, sin, gate_up, down,
+    sizes, cols, query, kv_all, bias, logsum, mixed, dnormed_part, mlp_part, hidden, cot, att, normed_all,
+    mixed_all, inputs, gain, mlp_gain, cos, sin, gate_up, down,
 ):
     dp, gx, gy = sizes
     q_cols, k_cols, v_cols, o_cols = cols
@@ -632,12 +643,14 @@
 
     def kernel(net, *refs):
         (
-            q_ref, kv_ref, bias_ref, logsum_ref, mixed_ref, dmixed_ref, dhidden_ref, att_ref, nm_ref,
-            mx_ref, in_ref, gain_ref, mlpgain_ref, cos_ref, sin_ref, gu_ref, dn_ref,
-        ) = refs[:17]
-        input_grad, gu_out, dn_out, att_out, gain_out = refs[17:22]
-        q_wide, k_wide, dkv_ref, p_ref, trade_src, trade_in, dn_one, att_grad, gains = refs[22:31]
-        refs = refs[31:]
+            q_ref, kv_ref, bias_ref, logsum_ref, mixed_ref, two_ref, mo_ref, hidden_ref, cot_ref, att_ref,
+            nm_ref, mx_ref, in_ref, gain_ref, two_gain_ref, cos_ref, sin_ref, gu_ref, dn_ref,
+        ) = refs[:19]
+        layer_out, input_grad, gu_out, dn_out, att_out, gain_out = refs[19:25]
+        q_wide, k_wide, dkv_ref, p_ref, trade_src, trade_in, dn_one, att_grad, gains = refs[25:34]
+        dmixed_ref, dhidden_ref = refs[34:36]
+        two_scratch, mo_scratch = refs[36:40], refs[40:44]
+        refs = refs[44:]
         landing_x, stage, landing_y = (refs[n * count : (n + 1) * count] for n in range(3))
         result, sems = refs[3 * count : 4 * count - 1], refs[4 * count - 1]
 
@@ -676,21 +689,42 @@
                 own.append(pltpu.make_async_copy(result[n], shares[n].out(net.d), sems.at[n]))
                 own[-1].start()
 
-        begin(mlp_sums, order[:1])
+        two_sum, mo_sum = TokenSum(net, two_ref, *two_scratch), TokenSum(net, mo_ref, *mo_scratch)
+        two_sum.start()
+        begin(mlp_sums, order[:2])
+        two_sum.relay()
+        mo_sum.start()
+        hidden = hidden_ref[...]
+        rms_two = lax.rsqrt(jnp.sum(hidden * hidden, axis=1, keepdims=True) / width + EPSILON)
+        unit_two = hidden * rms_two
+        dnormed_two = two_sum.total()
+        scaled_two = dnormed_two * two_gain_ref[...]
+        level_two = jnp.sum(scaled_two * unit_two, axis=1, keepdims=True) / width
+        dhidden_ref[...] = cot_ref[...].astype(F32) + rms_two * (scaled_two - unit_two * level_two)
+        gains[...] = jnp.zeros_like(gains)
+        gains[1:2, :] = jnp.sum(dnormed_two * unit_two, axis=0, keepdims=True)
+        mo_sum.relay()
+        dhidden_bf = dhidden_ref[...].astype(BF16)
+        for a in range(gx):
+            dmixed_ref[:, a * fan : (a + 1) * fan] = sum(
+                plain_product(dhidden_bf[:, b * o_cols : (b + 1) * o_cols], att_ref[a, b, qkv_cols:, :])
+                for b in range(gy)
+            ).astype(BF16)
+        relay(mlp_sums, order[:1])
         q_wide[...] = jnp.zeros_like(q_wide)
         k_wide[...] = jnp.zeros_like(k_wide)
         attend_heads_back(
             q_ref, kv_ref, bias_ref, logsum_ref, mixed_ref, dmixed_ref, q_wide, dkv_ref
         )
         begin([dkv_sum], order)
-        begin(mlp_sums, order[1:2])
-        relay(mlp_sums, order[:1])
+        begin(mlp_sums, order[2:3])
+        relay(mlp_sums, order[1:2])
+        layer_out[...] = (hidden_ref[...] + mo_sum.total()).astype(BF16)
         relay([dkv_sum], order)
-        begin(mlp_sums, order[2:])
+        begin(mlp_sums, order[3:])
         cos_rows, sin_rows = cos_ref[...], -sin_ref[...]
         dquery = turn_pairs(q_wide[...], cos_rows, sin_rows)[:, :q_width].astype(BF16)
         dhidden = dhidden_ref[...]
-        dhidden_bf = dhidden.astype(BF16)
         for b in range(gy):
             p_ref[b, :, :q_cols] = dquery[:, b * q_cols : (b + 1) * q_cols]
             p_ref[b, :, qkv_cols:] = dhidden_bf[:, b * o_cols : (b + 1) * o_cols]
@@ -711,7 +745,7 @@
             rank = lax.rem(net.d + i, dp)
             net.send(trade_src.at[rank], trade_in.at[net.d], trade_slot + net.d, net.dp_peer(i))
         trade_in[net.d] = trade_src[net.d]
-        relay(mlp_sums, order[1:2])
+        relay(mlp_sums, order[2:3])
 
         for a in range(gx):
             dn_one[:, a * fan : (a + 1) * fan] = sum(
@@ -724,9 +758,7 @@
         scaled = dnormed * gain_ref[...]
         level = jnp.sum(scaled * unit, axis=1, keepdims=True) / width
         input_grad[...] = (dhidden + rms * (scaled - unit * level)).astype(BF16)
-        gains[...] = jnp.zeros_like(gains)
         gains[0:1, :] = jnp.sum(dnormed * unit, axis=0, keepdims=True)
-        gains[1:2, :] = mlpgain_ref[...]
 
         for i in range(1, dp):
             rank = lax.rem(net.d + i, dp)
@@ -744,7 +776,7 @@
             for b in range(gy):
                 att_grad[a, b] = grad[b * att_share : (b + 1) * att_share]
         begin(att_sums, order)
-        relay(mlp_sums, order[2:])
+        relay(mlp_sums, order[3:])
         finish(0, mlp_sums)
         relay(att_sums, order)
         finish(3, att_sums)
@@ -755,6 +787,7 @@
         wait_local(own)
 
     shapes = (
+        jax.ShapeDtypeStruct(inputs.shape, BF16),
         jax.ShapeDtypeStruct(inputs.shape, BF16),
         jax.ShapeDtypeStruct((dp, 2) + pieces[0][0], BF16),
         jax.ShapeDtypeStruct((dp,) + pieces[2][0], BF16),
@@ -771,17 +804,21 @@
         pltpu.VMEM((rows, width), F32),
         pltpu.VMEM((gx, gy, att_share, fan), BF16),
         pltpu.VMEM((8, width), F32),
+        pltpu.VMEM((rows, width), BF16),
+        pltpu.VMEM((rows, width), F32),
     ]
+    slab = pltpu.VMEM((dp // 2, rows, width), BF16)
+    scratch += [pltpu.VMEM((2, rows, width), BF16), slab, slab, pltpu.SemaphoreType.DMA((2,))] * 2
     scratch += [pltpu.VMEM((gx, gy) + p, t) for p, t in pieces]
     scratch += [pltpu.VMEM((gy,) + p, t) for p, t in pieces] * 2
     scratch += [pltpu.VMEM(p, t) for p, t in pieces[:-1]]
     scratch += [pltpu.SemaphoreType.DMA((count - 1,))]
-    sems = count * (gx * gy + gy) + (count - 1) * 2 * dp + dp
+    sems = count * (gx * gy + gy) + (count - 1) * 2 * dp + 3 * dp
     return call(
-        kernel, sizes, 5, "backward", shapes, [VMEM] + [ANY] * 4, [VMEM] * 17, scratch, sems, sems,
+        kernel, sizes, 5, "backward", shapes, [VMEM] * 2 + [ANY] * 4, [VMEM] * 5 + [ANY] * 2 + [VMEM] * 12, scratch, sems, sems,
     )(
-        query, kv_all, bias, logsum, mixed, dmixed, dhidden, att, normed_all, mixed_all,
-        inputs, gain, mlpgain, cos, sin, gate_up, down,
+        query, kv_all, bias, logsum, mixed, dnormed_part, mlp_part, hidden, cot, att, normed_all,
+        mixed_all, inputs, gain, mlp_gain, cos, sin, gate_up, down,
     )
 
 
@@ -796,12 +833,6 @@
     rms_rows = lax.rsqrt(jnp.mean(values * values, axis=1, keepdims=True) + EPSILON)
     unit_rows = values * rms_rows
     return (rms_rows, unit_rows, (unit_rows * gain).astype(BF16))
-
-
-def normalize_back(dnormed, gain, rms_rows, unit_rows):
-    scaled = dnormed * gain
-    dvalues = rms_rows * (scaled - unit_rows * jnp.mean(scaled * unit_rows, axis=1, keepdims=True))
-    return (dvalues, jnp.sum(dnormed * unit_rows, axis=0))
 
 
 def on_device(
@@ -855,17 +886,17 @@
         down_weight.reshape(groups, dp, share, down_cols), rank, 1, 1
     ).reshape(groups * share, down_cols).T
 
-    att_all = gather_weights(sizes, att_part).reshape(gx, gy, all_cols, fan)
+    att_all, gate_up_all = gather_weights(sizes, att_part, gate_up_part)
+    att_all = att_all.reshape(gx, gy, all_cols, fan)
     cos_wide = jnp.tile(cos_table[:, 0], (1, 4))
     sin_wide = jnp.tile(jnp.concatenate([-sin_table[:, 0], sin_table[:, 0]], axis=1), (1, 2))
     (
         rotated_query, kv_all, attention_mixture, logsum, hidden,
-        gate_up_all, down_all, cot_all, normed_one_all, mixed_all, normed_all,
+        down_all, cot_all, normed_one_all, mixed_all, normed_all,
     ) = forward(
         sizes, (q_cols, k_cols, v_cols, o_cols), att_all, normed_one, inputs, mlp_gain.reshape(1, -1),
-        cos_wide, sin_wide, bias, gate_up_part, down_part, cotangent,
-    )
-    out_rows = att_all[:, :, qkv_cols:].reshape(gx, gy * o_cols, fan)
+        cos_wide, sin_wide, bias, down_part, cotangent,
+    )
     hidden_width = gy * share
     gate_up_all = gate_up_all.reshape(gx, 2 * hidden_width, fan)
     half_hidden = groups * share
@@ -873,33 +904,15 @@
     cot_all, normed_one_all, mixed_all, normed_all = (
         rows.reshape(dp * count_of_rows, width) for rows in (cot_all, normed_one_all, mixed_all, normed_all)
     )
-    rms_two, unit_two, _ = normalize(hidden, mlp_gain)
-
-    def parts(rows):
-        return [rows[:, a * fan : (a + 1) * fan] for a in range(gx)]
-
-    def back_onto(rows, weights):
-        return jnp.concatenate([plain_product(rows, weights[a]) for a in range(gx)], axis=1)
-
     dnormed_part, mlp_part, gate_up_grad, down_grad = mlp(normed_all, cot_all, gate_up_all, down_all)
-    dnormed_two, mlp_out = sum_tokens(
-        sizes,
-        dnormed_part.reshape(dp, count_of_rows, width),
-        mlp_part.reshape(dp, count_of_rows, width),
-    )
-    layer_out = (hidden + mlp_out).astype(BF16)
-
     gate_up_grad = gate_up_grad.reshape(gx, 2, gy, share, fan)
     down_grad = down_grad.reshape(gx, gy, down_cols, half_hidden)
 
-    dhidden_norm, mlpgain_part = normalize_back(dnormed_two, mlp_gain, rms_two, unit_two)
-    dhidden = cotangent.astype(F32) + dhidden_norm
-    dhidden_bf = dhidden.astype(BF16)
-    mixture_gradient = back_onto(dhidden_bf, out_rows).astype(BF16)
-    input_grad, gate_up_sum, down_sum, att_sum, gain_sum = backward(
+    layer_out, input_grad, gate_up_sum, down_sum, att_sum, gain_sum = backward(
         sizes, (q_cols, k_cols, v_cols, o_cols), rotated_query, kv_all, bias, logsum, attention_mixture,
-        mixture_gradient, dhidden, att_all, normed_one_all, mixed_all, inputs, attn_gain.reshape(1, -1),
-        mlpgain_part.reshape(1, -1), cos_wide, sin_wide, gate_up_grad, down_grad,
+        dnormed_part.reshape(dp, count_of_rows, width), mlp_part.reshape(dp, count_of_rows, width),
+        hidden, cotangent, att_all, normed_one_all, mixed_all, inputs, attn_gain.reshape(1, -1),
+        mlp_gain.reshape(1, -1), cos_wide, sin_wide, gate_up_grad, down_grad,
     )
     gate_grad = gate_up_sum[:, 0].reshape(dp * share, fan).T.astype(F32)
     up_grad = gate_up_sum[:, 1].reshape(dp * share, fan).T.astype(F32)

time: 316 us -> 292 us (0.924); the launches traced: 315 us -> 287 us
  Pallas kernels: 285 us -> 261 us
    pallas_call x4 -> x3, Pallas kernels: 272 us -> 249 us  [the longest x1 116 us: backward(): call(kernel, sizes, 5, 'backward', shapes, [VMEM] * 2 + [ANY] * 4, [VMEM]...]
    unnamed x50 -> x36, local copies, waits for them, and re-layouts: 6.53 us -> 9.39 us
where the time goes in v3:
time: 292 us; the launch traced here: 287 us
  Pallas kernels  261 us (89%)
  local copies, waits for them, and re-layouts  19.5 us (7%)
  other arithmetic  5.56 us (2%)
    pallas_call x1, Pallas kernels, backward(): call(kernel, sizes, 5, 'backward', shapes, [VMEM] * 2 + [ANY] * 4, [VMEM]...  116 us
    pallas_call x1, Pallas kernels, forward(): call(kernel, sizes, 2, 'forward', shapes, [VMEM] * 5 + [ANY] * 5, [VMEM]...  71.4 us
    pallas_call x1, Pallas kernels, gather_weights(): call(kernel, sizes, 1, 'gather_weights', shapes, [ANY] * 2, [VMEM] * 2, [...  61.2 us
    pallas_call x1, Pallas kernels, mlp(): pl.pallas_call(kernel, name='mlp', out_shape=(jax.ShapeDtypeStruct(normed...  12.8 us
    unnamed x36, local copies, waits for them, and re-layouts  9.39 us

profile of v3, /device:TPU:31, one launch (start us, length us, event | category | flops | bytes accessed | tf_op | source)
XLA Modules:
  0.0 287.3 jit_solution(8915667195385058604)
XLA Ops:
  0.7 0.9 dynamic_slice.18
  1.8 0.7 copy.50.refs_5_.refs_16_
  2.5 0.7 copy.49.refs_4_.refs_15_
  3.2 1.1 copy.41
  4.5 1.1 fusion.8.refs_0_
  6.0 0.8 fusion.2.refs_1_
  6.8 0.8 copy.51.refs_8_
  7.6 1.3 constant_dynamic-slice_fusion.1
  9.2 0.8 pad_maximum_fusion.refs_1_
  10.0 1.0 fusion.4.refs_6_.refs_2_
  11.3 0.8 copy.47
  12.1 61.2 %gather_weights.1 = (bf16[2,4,4,160,480]{4,3,2,1,0:T(8,128)(2,1)}, bf16[2,2,4,160,480]{4,3,2,1,0:T(8,128)(2,1)}) custom-call(bf16[160,480]{1,0:T(8,128)(2,1)} %fusion.8.refs_0_, bf16[2,160,480]{2,1,0:T(8,128)(2,1)} %pad_maximum_fusion.refs_1_), custom_call_target="tpu_custom_call" | custom-call | tf_op jit(solution)/shard_map/gather_weights/pallas_call | solution.py:380
  73.3 71.4 %forward.1 = (bf16[128,960]{1,0:T(8,128)(2,1)}, bf16[2,4,128,640]{3,2,1,0:T(8,128)(2,1)}, bf16[128,960]{1,0:T(8,128)(2,1)}, f32[5,384]{1,0:T(8,128)}, f32[128,96...) custom-call(bf16[2,4,640,480]{3,2,1,0:T(8,128)(2,1)} %bitcast.44, ...), custom_call_target="tpu_custom_call" | custom-call | tf_op jit(solution)/shard_map/forward/pallas_call | solution.py:567
  144.8 12.8 %mlp.1 = (bf16[512,960]{1,0:T(8,128)(2,1)}, bf16[512,960]{1,0:T(8,128)(2,1)}, bf16[2,1280,480]{2,1,0:T(8,128)(2,1)}, bf16[2,960,320]{2,1,0:T(8,128)(2,1)}) custom-call(bf16[512,960]{1,0:T(8,128)(2,1)} %bitcast.61, bf16[512,960]{1,0:T(8,128)(2,1)} %bitcast.60, bf16[2,1280,480]{2,1,0:T(8,128)(2,1)} %bitcast.50, bf16[2,960,320]{2,1,0:T(8,128)(2,1)} %bitcast.52), custom_call_target="tpu_custom_call" | custom-call | tf_op jit(solution)/shard_map/mlp/pallas_call | solution.py:608
  157.6 115.9 %backward.1 = (bf16[128,960]{1,0:T(8,128)(2,1)}, bf16[128,960]{1,0:T(8,128)(2,1)}, bf16[4,2,160,480]{3,2,1,0:T(8,128)(2,1)}, bf16[4,240,320]{2,1,0:T(8,128)(2,1)...) custom-call(bf16[128,960]{1,0:T(8,128)(2,1)} %get-tuple-element.34.refs_0_, ...), custom_call_target="tpu_custom_call" | custom-call | tf_op jit(solution)/shard_map/backward/pallas_call | solution.py:817
  273.5 1.9 copy.61
  275.4 0.9 reduce_sum.19
  276.9 1.8 copy.62
  279.5 1.1 fusion.12
  280.6 0.8 copy.64
  281.4 0.8 copy.63
  282.5 1.4 copy.65
  284.3 1.4 copy.58
  285.9 1.4 copy.57
  (47 shorter events, 3.4 us)
Async XLA Ops:
  0.6 3.7 %copy-start.5 = (bf16[480,240]{1,0:T(8,128)(2,1)S(1)}, bf16[480,240]{1,0:T(8,128)(2,1)}, u32[]{:S(2)}) copy-start(bf16[480,240]{1,0:T(8,128)(2,1)} %param.18) | copy-start | bytes 691204
  0.7 3.8 %copy-start.9 = (bf16[480,80]{0,1:T(8,128)(2,1)S(1)}, bf16[480,80]{0,1:T(8,128)(2,1)}, u32[]{:S(2)}) copy-start(bf16[480,80]{0,1:T(8,128)(2,1)} %param.17) | copy-start | bytes 230404
  0.7 3.8 %copy-start.8 = (bf16[480,80]{0,1:T(8,128)(2,1)S(1)}, bf16[480,80]{0,1:T(8,128)(2,1)}, u32[]{:S(2)}) copy-start(bf16[480,80]{0,1:T(8,128)(2,1)} %param.16) | copy-start | bytes 230404
  0.7 5.0 %copy-start.6 = (bf16[128,960]{0,1:T(8,128)(2,1)S(1)}, bf16[128,960]{0,1:T(8,128)(2,1)}, u32[]{:S(2)}) copy-start(bf16[128,960]{0,1:T(8,128)(2,1)} %param.12) | copy-start | bytes 737284
  3.2 2.7 copy-start.10
  4.3 2.5 copy-start.7
  5.8 3.3 %copy-start = (bf16[128,960]{1,0:T(8,128)(2,1)}, bf16[128,960]{1,0:T(8,128)(2,1)S(1)}, u32[]{:S(2)}) copy-start(bf16[128,960]{1,0:T(8,128)(2,1)S(1)} %copy.45.refs_2_.refs_12_) | copy-start | bytes 737284
  7.6 2.4 copy-start.11
  7.6 3.4 %copy-start.4 = (bf16[1280,240]{0,1:T(8,128)(2,1)S(1)}, bf16[1280,240]{0,1:T(8,128)(2,1)}, u32[]{:S(2)}) copy-start(bf16[1280,240]{0,1:T(8,128)(2,1)} %param.22) | copy-start | bytes 1843204
  273.5 5.2 %copy-start.3 = (bf16[4,160,480]{2,1,0:T(8,128)(2,1)S(1)}, bf16[4,160,480]{2,1,0:T(8,128)(2,1)}, u32[]{:S(2)}) copy-start(bf16[4,160,480]{2,1,0:T(8,128)(2,1)} %get-tuple-element.51) | copy-start | bytes 1843204
  279.5 2.7 copy-start.2
  282.5 1.4 copy-start.1

commit v4 on v3

--- a/solution.py
+++ b/solution.py
@@ -350,7 +350,7 @@
         shared(net.x, net.y).start(att_ref)
         gu_plane.start_gy()
         local(own)
-        for k in range(1, gy):
+        for k in range(gy - 1, 0, -1):
             att_plane.relay(k)
             row = net.at_gy(k)
             shared(net.x, row).start(att_out.at[net.x, row, net.d])
@@ -364,7 +364,7 @@
         for n, (j, k) in enumerate(places):
             shared(net.at_gx(j), net.at_gy(k)).relay()
             if n % 2 == 1 and n // 2 + 1 < gy:
-                gu_plane.relay(n // 2 + 1)
+                gu_plane.relay(gy - 1 - n // 2)
         for j, k in places:
             shared(net.at_gx(j), net.at_gy(k)).settle()
         for j in range(1, gx):
@@ -504,7 +504,7 @@
         cot_share.start(cot_ref)
         nm_share.start(nm_ref)
         q_ref[...] = turn_pairs(q_wide[...], cos_rows, sin_rows)[:, :q_width].astype(BF16)
-        for k in range(1, gy):
+        for k in range(gy - 1, 0, -1):
             kv.relay(k)
         dn.start_gx()
         for j in range(1, gx):
@@ -512,7 +512,7 @@
                 kv.settle(j, k)
         wait_local(own)
 
-        turns = list(range(1, gy))
+        turns = list(range(gy - 1, 0, -1))
         heads = list(range(KEY_VALUE_HEADS))
         for n, k in enumerate(turns):
             mine = heads[n * len(heads) // len(turns) : (n + 1) * len(heads) // len(turns)]

time: 292 us -> 283 us (0.969)
  Pallas kernels: 261 us -> 253 us
    pallas_call x1, Pallas kernels: 71.4 us -> 64.4 us  [forward(): call(kernel, sizes, 2, 'forward', shapes, [VMEM] * 5 + [ANY] * 5, [VMEM]...]
where the time goes in v4:
time: 283 us; the launch traced here: 279 us
  Pallas kernels  253 us (89%)
  local copies, waits for them, and re-layouts  19.5 us (7%)
  other arithmetic  5.56 us (2%)
    pallas_call x1, Pallas kernels, backward(): call(kernel, sizes, 5, 'backward', shapes, [VMEM] * 2 + [ANY] * 4, [VMEM]...  114 us
    pallas_call x1, Pallas kernels, forward(): call(kernel, sizes, 2, 'forward', shapes, [VMEM] * 5 + [ANY] * 5, [VMEM]...  64.4 us
    pallas_call x1, Pallas kernels, gather_weights(): call(kernel, sizes, 1, 'gather_weights', shapes, [ANY] * 2, [VMEM] * 2, [...  61.2 us
    pallas_call x1, Pallas kernels, mlp(): pl.pallas_call(kernel, name='mlp', out_shape=(jax.ShapeDtypeStruct(normed...  12.8 us
    unnamed x36, local copies, waits for them, and re-layouts  9.39 us

profile of v4, /device:TPU:31, one launch (start us, length us, event | category | flops | bytes accessed | tf_op | source)
XLA Modules:
  0.0 278.7 jit_solution(6661821807782351487)
XLA Ops:
  0.7 0.9 dynamic_slice.18
  1.8 0.7 copy.50.refs_5_.refs_16_
  2.5 0.7 copy.49.refs_4_.refs_15_
  3.2 1.1 copy.41
  4.5 1.1 fusion.8.refs_0_
  6.0 0.8 fusion.2.refs_1_
  6.8 0.8 copy.51.refs_8_
  7.6 1.3 constant_dynamic-slice_fusion.1
  9.2 0.8 pad_maximum_fusion.refs_1_
  10.0 1.0 fusion.4.refs_6_.refs_2_
  11.3 0.8 copy.47
  12.1 61.2 %gather_weights.1 = (bf16[2,4,4,160,480]{4,3,2,1,0:T(8,128)(2,1)}, bf16[2,2,4,160,480]{4,3,2,1,0:T(8,128)(2,1)}) custom-call(bf16[160,480]{1,0:T(8,128)(2,1)} %fusion.8.refs_0_, bf16[2,160,480]{2,1,0:T(8,128)(2,1)} %pad_maximum_fusion.refs_1_), custom_call_target="tpu_custom_call" | custom-call | tf_op jit(solution)/shard_map/gather_weights/pallas_call | solution.py:380
  73.3 64.4 %forward.1 = (bf16[128,960]{1,0:T(8,128)(2,1)}, bf16[2,4,128,640]{3,2,1,0:T(8,128)(2,1)}, bf16[128,960]{1,0:T(8,128)(2,1)}, f32[5,384]{1,0:T(8,128)}, f32[128,96...) custom-call(bf16[2,4,640,480]{3,2,1,0:T(8,128)(2,1)} %bitcast.44, ...), custom_call_target="tpu_custom_call" | custom-call | tf_op jit(solution)/shard_map/forward/pallas_call | solution.py:567
  137.8 12.8 %mlp.1 = (bf16[512,960]{1,0:T(8,128)(2,1)}, bf16[512,960]{1,0:T(8,128)(2,1)}, bf16[2,1280,480]{2,1,0:T(8,128)(2,1)}, bf16[2,960,320]{2,1,0:T(8,128)(2,1)}) custom-call(bf16[512,960]{1,0:T(8,128)(2,1)} %bitcast.61, bf16[512,960]{1,0:T(8,128)(2,1)} %bitcast.60, bf16[2,1280,480]{2,1,0:T(8,128)(2,1)} %bitcast.50, bf16[2,960,320]{2,1,0:T(8,128)(2,1)} %bitcast.52), custom_call_target="tpu_custom_call" | custom-call | tf_op jit(solution)/shard_map/mlp/pallas_call | solution.py:608
  150.6 114.3 %backward.1 = (bf16[128,960]{1,0:T(8,128)(2,1)}, bf16[128,960]{1,0:T(8,128)(2,1)}, bf16[4,2,160,480]{3,2,1,0:T(8,128)(2,1)}, bf16[4,240,320]{2,1,0:T(8,128)(2,1)...) custom-call(bf16[128,960]{1,0:T(8,128)(2,1)} %get-tuple-element.34.refs_0_, ...), custom_call_target="tpu_custom_call" | custom-call | tf_op jit(solution)/shard_map/backward/pallas_call | solution.py:817
  264.8 1.9 copy.61
  266.7 0.9 reduce_sum.19
  268.2 1.8 copy.62
  270.8 1.1 fusion.12
  271.9 0.8 copy.64
  272.7 0.8 copy.63
  273.9 1.4 copy.65
  275.6 1.4 copy.58
  277.2 1.4 copy.57
  (47 shorter events, 3.4 us)
Async XLA Ops:
  0.6 3.7 %copy-start.5 = (bf16[480,240]{1,0:T(8,128)(2,1)S(1)}, bf16[480,240]{1,0:T(8,128)(2,1)}, u32[]{:S(2)}) copy-start(bf16[480,240]{1,0:T(8,128)(2,1)} %param.18) | copy-start | bytes 691204
  0.7 3.8 %copy-start.9 = (bf16[480,80]{0,1:T(8,128)(2,1)S(1)}, bf16[480,80]{0,1:T(8,128)(2,1)}, u32[]{:S(2)}) copy-start(bf16[480,80]{0,1:T(8,128)(2,1)} %param.17) | copy-start | bytes 230404
  0.7 3.8 %copy-start.8 = (bf16[480,80]{0,1:T(8,128)(2,1)S(1)}, bf16[480,80]{0,1:T(8,128)(2,1)}, u32[]{:S(2)}) copy-start(bf16[480,80]{0,1:T(8,128)(2,1)} %param.16) | copy-start | bytes 230404
  0.7 5.0 %copy-start.6 = (bf16[128,960]{0,1:T(8,128)(2,1)S(1)}, bf16[128,960]{0,1:T(8,128)(2,1)}, u32[]{:S(2)}) copy-start(bf16[128,960]{0,1:T(8,128)(2,1)} %param.12) | copy-start | bytes 737284
  3.2 2.7 copy-start.10
  4.3 2.5 copy-start.7
  5.8 3.3 %copy-start = (bf16[128,960]{1,0:T(8,128)(2,1)}, bf16[128,960]{1,0:T(8,128)(2,1)S(1)}, u32[]{:S(2)}) copy-start(bf16[128,960]{1,0:T(8,128)(2,1)S(1)} %copy.45.refs_2_.refs_12_) | copy-start | bytes 737284
  7.6 2.4 copy-start.11
  7.6 3.4 %copy-start.4 = (bf16[1280,240]{0,1:T(8,128)(2,1)S(1)}, bf16[1280,240]{0,1:T(8,128)(2,1)}, u32[]{:S(2)}) copy-start(bf16[1280,240]{0,1:T(8,128)(2,1)} %param.22) | copy-start | bytes 1843204
  264.8 5.2 %copy-start.3 = (bf16[4,160,480]{2,1,0:T(8,128)(2,1)S(1)}, bf16[4,160,480]{2,1,0:T(8,128)(2,1)}, u32[]{:S(2)}) copy-start(bf16[4,160,480]{2,1,0:T(8,128)(2,1)} %get-tuple-element.51) | copy-start | bytes 1843204
  270.8 2.7 copy-start.2
  273.9 1.4 copy-start.1
